TPU v7x, 256 devices: a whole 4x4x8 slice. The times are simulated.
256 devices in a mesh: col: 32 (over x_hi, z, core), row: 8 (over x_lo, y).
Axes of the slice: x: 4 (x_hi: 2, x_lo: 2; x = x_hi * 2 + x_lo), y: 4, z: 8, core: 2. Of those that a mesh axis runs over, the one named last changes fastest.
Arguments:
- matrix: float32 [64, 64, 128, 128], P('col', 'row'), may hold values from -12 to 80, as said below
- col_owner: int32 [64], replicated, may hold values from 0 to 63, as said below
- row_owner: int32 [64], replicated, may hold values from 0 to 63, as said below
- pattern: int32 [2, 64], replicated, may hold values from 0 to 1, as said below
Outputs:
- factored: float32 [64, 64, 128, 128], P('col', 'row')
Inputs may be any that keep to these rules, and one draw needn't show every extreme that they name: `col_owner`: a permutation of 0 to 63. `row_owner`: a permutation of 0 to 63. pattern[0, 1] is 1; pattern[k, i] is 0 for i <= k; pattern[1, i] >= pattern[0, i] for every i >= 2. `matrix`: the diagonal tile of every supernode is symmetric positive definite, and so is every diagonal tile after the updates.
All inputs are finite; a program needn't handle non-finite values.
Results may differ from a plain program's by a relative error of at most 0.0003.
Values sent between devices are 32-bit elements; how exact they have to be, the bound alone decides.
A program may use at most 64 MiB of HBM per device.

v0:
```python
import jax
import jax.numpy as jnp
from jax import lax
from jax.sharding import PartitionSpec as P

PRECISE = lax.Precision.HIGHEST


def broadcast(block, axis, source):
    block = jnp.where(lax.axis_index(axis) == source, block, jnp.zeros_like(block))
    return lax.psum(block, axis)


def owned_nodes(owner_map, first_place, how_many):
    places = first_place + jnp.arange(how_many, dtype=jnp.int32)
    ordinal = jnp.arange(owner_map.shape[0], dtype=jnp.int32)
    matches = owner_map[None, :] == places[:, None]
    return jnp.sum(jnp.where(matches, ordinal[None, :], 0), axis=1)


def diag_factor(diag_tile):
    lower_tri = jnp.linalg.cholesky(diag_tile)
    identity = jnp.eye(lower_tri.shape[0], dtype=lower_tri.dtype)
    return (lower_tri, lax.linalg.triangular_solve(lower_tri, identity, left_side=True, lower=True))


def solve_rows(tile_rows, inverse, kept_rows):
    scaled = jnp.einsum("spq,rq->spr", tile_rows, inverse, precision=PRECISE)
    return jnp.where(kept_rows[:, None, None], scaled, jnp.zeros_like(scaled))


def schur_apply(matrix, row_factors, col_factors, row_node, col_node):
    product = jnp.einsum("spq,lrq->lspr", row_factors, col_factors, precision=PRECISE)
    lower_half = row_node[None, :] >= col_node[:, None]
    return matrix - jnp.where(lower_half[:, :, None, None], product, jnp.zeros_like(product))


def write_back(matrix, local_col, is_owner, lower_tri, row_factors, kept_rows, row_node, panel_id):
    old_column = lax.dynamic_index_in_dim(matrix, local_col, 0, keepdims=False)
    is_diag = row_node == panel_id
    new_column = jnp.where(
        is_diag[:, None, None],
        lower_tri[None],
        jnp.where(kept_rows[:, None, None], row_factors, old_column),
    )
    new_column = jnp.where(is_owner, new_column, old_column)
    return lax.dynamic_update_index_in_dim(matrix, new_column, local_col, 0)


def body(matrix, col_owner, row_owner, pattern):
    cols_here = matrix.shape[0]
    slots_here = matrix.shape[1]
    col_rank = lax.axis_index("col")
    row_rank = lax.axis_index("row")
    first_slot = row_rank * slots_here
    col_node = owned_nodes(col_owner, col_rank * cols_here, cols_here)
    row_node = owned_nodes(row_owner, first_slot, slots_here)
    source_slot = row_owner[col_node]
    for panel_id in range(2):
        position = col_owner[panel_id]
        owner_col = position // cols_here
        local_col = position % cols_here
        diag_slot = row_owner[panel_id]
        kept_rows = pattern[panel_id][row_node] == 1
        kept_cols = pattern[panel_id][col_node] == 1
        raw_column = lax.dynamic_index_in_dim(matrix, local_col, 0, keepdims=False)
        gathered = lax.all_gather(raw_column, "row", axis=0, tiled=True)
        whole_column = broadcast(gathered, "col", owner_col)
        lower_tri, inverse = diag_factor(
            lax.dynamic_index_in_dim(whole_column, diag_slot, 0, keepdims=False)
        )
        my_rows = lax.dynamic_slice_in_dim(whole_column, first_slot, slots_here, 0)
        row_factors = solve_rows(my_rows, inverse, kept_rows)
        col_factors = solve_rows(jnp.take(whole_column, source_slot, axis=0), inverse, kept_cols)
        matrix = schur_apply(matrix, row_factors, col_factors, row_node, col_node)
        matrix = write_back(
            matrix,
            local_col,
            col_rank == owner_col,
            lower_tri,
            row_factors,
            kept_rows,
            row_node,
            panel_id,
        )
    return matrix


def solution(mesh):
    return jax.shard_map(
        body,
        mesh=mesh,
        in_specs=(P("col", "row", None, None), P(), P(), P()),
        out_specs=P("col", "row", None, None),
        check_vma=False,
    )
```

profile of v0, /device:TPU:1, one launch (start us, length us, event | category | flops | bytes accessed | tf_op | source)
XLA Modules:
  0.0 760.7 jit_solution(656796158354332296)
XLA Ops:
  6.5 0.0 all-gather.5.cloned.1.call-start
  6.5 1.3 fusion.38
  10.0 1.9 dynamic-slice_bitcast_fusion
  11.8 0.0 all-gather.5.cloned.1.call-update
  11.9 0.0 all-reduce.3.cloned.1.call-start
  12.6 58.3 %all-gather.5.cloned.1.call-done = f32[1,64,128,128]{3,2,0,1:T(8,128)} async-done(((f32[1,8,128,128]{3,2,0,1:T(8,128)}), f32[1,64,128,128]{3,2,0,1:T(8,128)}) %all-gather.5.cloned.1.call-update) | async-done | bytes 4194320 | tf_op jit(solution)/shard_map/all_gather | solution.py:67
  71.0 4.7 fusion.1
  75.6 0.0 copy-start
  75.6 0.0 copy-start.1
  75.6 0.0 all-reduce.3.cloned.1.call-update
  75.7 0.0 all-gather.7.cloned.1.call-start
  77.5 0.0 copy-done
  77.5 0.6 fusion.37
  79.4 0.0 copy-done.1
  79.4 0.3 copy.35
  79.8 0.0 copy-done.2
  79.8 0.2 fusion.31
  80.0 0.6 gather_fusion.1
  80.6 0.0 copy-done.3
  80.6 0.6 gather_fusion
  81.3 0.2 select_reduce_fusion.2
  81.5 0.6 gather_fusion.2
  82.8 0.1 broadcast_compare_fusion
  82.9 270.1 %all-reduce.3.cloned.1.call-done = f32[64,128,128]{2,1,0:T(8,128)} async-done(((f32[64,128,128]{2,1,0:T(8,128)}), f32[64,128,128]{2,1,0:T(8,128)}) %all-reduce.3.cloned.1.call-update) | async-done | bytes 4194320 | tf_op jit(solution)/shard_map/psum | solution.py:11
  353.0 0.8 constant_dynamic-slice_fusion.4
  353.8 0.1 copy.33
  353.9 0.9 fusion.21
  354.8 11.7 %cholesky.44 = f32[128,128]{1,0:T(8,128)S(1)} custom-call(f32[128,128]{1,0:T(8,128)S(1)} %fusion.21), custom_call_target="Cholesky" | custom-call | tf_op jit(solution)/shard_map/jit(cholesky)/cholesky | solution.py:22
  366.5 0.6 compare_reduce_fusion.1
  367.2 0.7 select_bitcast_fusion.1
  367.9 9.8 %custom-call.6 = f32[1,128,128]{1,2,0:T(8,128)S(1)} custom-call(f32[1,128,128]{2,1,0:T(8,128)S(1)} %get-tuple-element.10), custom_call_target="InvertDiagBlocksLowerTriangular" | custom-call | tf_op jit(solution)/shard_map/triangular_solve/custom-call.0 | solution.py:24
  377.7 0.3 convolution_bitcast_fusion.1
  378.0 2.7 gather_fusion.5
  380.7 0.3 fusion.7
  381.0 1.6 convolution_select_fusion.3
  382.7 1.0 fusion.3
  383.7 0.2 copy.36
  384.0 0.2 fusion.12
  384.1 0.2 copy.37
  384.4 1.0 copy.38
  385.4 0.0 all-gather.7.cloned.1.call-update
  385.5 0.2 all-reduce.5.cloned.1.call-start
  386.3 53.1 %all-gather.7.cloned.1.call-done = f32[1,64,128,128]{3,2,0,1:T(8,128)} async-done(((f32[1,8,128,128]{3,2,0,1:T(8,128)}), f32[1,64,128,128]{3,2,0,1:T(8,128)}) %all-gather.7.cloned.1.call-update) | async-done | bytes 4194320 | tf_op jit(solution)/shard_map/all_gather | solution.py:67
  439.4 4.7 fusion
  444.0 0.0 all-reduce.5.cloned.1.call-update
  445.3 0.6 gather_fusion.3
  445.9 0.6 gather_fusion.4
  447.3 274.1 %all-reduce.5.cloned.1.call-done = f32[64,128,128]{2,1,0:T(8,128)} async-done(((f32[64,128,128]{2,1,0:T(8,128)}), f32[64,128,128]{2,1,0:T(8,128)}) %all-reduce.5.cloned.1.call-update) | async-done | bytes 4194320 | tf_op jit(solution)/shard_map/psum | solution.py:11
  721.4 0.8 constant_dynamic-slice_fusion.1
  722.2 0.1 copy.40
  722.3 0.9 fusion.20
  723.2 11.7 %cholesky.55 = f32[128,128]{1,0:T(8,128)S(1)} custom-call(f32[128,128]{1,0:T(8,128)S(1)} %fusion.20), custom_call_target="Cholesky" | custom-call | tf_op jit(solution)/shard_map/jit(cholesky)/cholesky | solution.py:22
  734.9 0.6 compare_reduce_fusion
  735.6 0.7 select_bitcast_fusion
  736.3 9.8 %custom-call.7 = f32[1,128,128]{1,2,0:T(8,128)S(1)} custom-call(f32[1,128,128]{2,1,0:T(8,128)S(1)} %get-tuple-element.6), custom_call_target="InvertDiagBlocksLowerTriangular" | custom-call | tf_op jit(solution)/shard_map/triangular_solve/custom-call.0 | solution.py:24
  746.1 0.3 convolution_bitcast_fusion
  746.4 2.7 gather_fusion.6
  749.1 0.3 fusion.6
  749.4 1.6 convolution_select_fusion.2
  751.1 1.0 fusion.5
  752.2 0.2 copy.42
  752.4 0.2 fusion.9
  752.6 0.2 copy.43
  752.8 1.3 copy.44
  (22 shorter events, 0.4 us)
Async XLA Ops:
  6.5 64.4 %all-gather.5.cloned.1.call-start = ((), (), s32[]{:S(2)}) async-start(), calls=%async_computation.2 | async-start | bytes 4718592 | tf_op jit(solution)/shard_map/all_gather | solution.py:67
  11.9 341.1 %all-reduce.3.cloned.1.call-start = ((), (), s32[]{:S(2)}) async-start(), calls=%async_computation | async-start | bytes 8388608 | tf_op jit(solution)/shard_map/psum | solution.py:11
  75.6 1.9 copy-start
  75.6 3.8 copy-start.1
  75.6 4.2 copy-start.2
  75.6 5.0 copy-start.3
  75.7 363.7 %all-gather.7.cloned.1.call-start = ((), (), s32[]{:S(2)}) async-start(), calls=%async_computation.3 | async-start | bytes 4718592 | tf_op jit(solution)/shard_map/all_gather | solution.py:67
  385.5 335.9 %all-reduce.5.cloned.1.call-start = ((), (), s32[]{:S(2)}) async-start(), calls=%async_computation.1 | async-start | bytes 8388608 | tf_op jit(solution)/shard_map/psum | solution.py:11
Sparse Core Ops, SparseCore 0:
  12.0 58.9 all-gather.4
  75.8 277.1 all-reduce.2
  385.6 53.7 all-gather.6
  444.2 277.1 all-reduce.4
where the time goes:
time: 761 us
  waiting for transfers between devices  656 us (86%)
  other arithmetic  57.6 us (8%)
  between operations  22.5 us (3%)
  local copies, waits for them, and re-layouts  18 us (2%)
    psum x2, waiting for transfers between devices, broadcast(): return lax.psum(block, axis)  544 us
    all_gather x2, waiting for transfers between devices, body(): gathered = lax.all_gather(raw_column, 'row', axis=0, tiled=True)  111 us
    another operation x6, other arithmetic, diag_factor(): lower_tri = jnp.linalg.cholesky(diag_tile)  24.8 us
    another operation x4, other arithmetic, diag_factor(): lax.linalg.triangular_solve(lower_tri, identity, left_side=True, lower=True)  20.9 us
  transfers between devices with their start and end apart: 4, of which 4 were waited for; matrix products, arithmetic and copies ran while one was open for 1% of the time, Pallas kernels for 0%

commit v1 on v0

v1 whole, which is shorter than its diff:
```python
import functools

import jax
import jax.numpy as jnp
from jax import lax
from jax.experimental import pallas as pl
from jax.experimental.pallas import tpu as pltpu
from jax.sharding import PartitionSpec as P

MESH = pl.DeviceIdType.MESH
F32 = jnp.float32
PRECISE = lax.Precision.HIGHEST
W = 128
NODES = 64


def my_place():
    col = lax.axis_index("col")
    row = lax.axis_index("row")
    return col // 16, (col // 2) % 8, col % 2, row // 4, row % 4


def device(xh, z, k, xl, y):
    return {"col": (xh * 8 + z) * 2 + k, "row": xl * 4 + y}


def send_all(count, me, source, slot, target, send_sem, recv_sem):
    def step(q, carry):
        @pl.when(q != me)
        def _():
            pltpu.make_async_remote_copy(
                src_ref=source(q),
                dst_ref=slot(me),
                send_sem=send_sem.at[q],
                recv_sem=recv_sem.at[me],
                device_id=target(q),
                device_id_type=MESH,
            ).start()

        return carry

    lax.fori_loop(0, count, step, 0)


def recv_all(count, me, source, slot, target, send_sem, recv_sem):
    def step(q, carry):
        @pl.when(q != me)
        def _():
            copy = pltpu.make_async_remote_copy(
                src_ref=source(q),
                dst_ref=slot(q),
                send_sem=send_sem.at[q],
                recv_sem=recv_sem.at[q],
                device_id=target(q),
                device_id_type=MESH,
            )
            copy.wait_send()
            copy.wait_recv()

        return carry

    lax.fori_loop(0, count, step, 0)


def comm_kernel(
    mat, co, ro, rows_out, cols_out, diag_out,
    st1, rc1, half, rc2, pc2, rows, cst, rc3, pc3, cols,
    dst1, rd1, pd1, rd2, pd2, diag,
    s1, r1, s2, r2, s4, r4, s5, r5, s6, r6, s7, r7, d1, e1, d2, e2, d3, e3,
):
    xh, z, k, xl, y = my_place()
    me_plane = (xh * 2 + xl) * 4 + y
    me_zk = z * 2 + k
    me_xz = xh * 8 + z
    me_row = xl * 4 + y

    def plane(q):
        return device(q // 8, z, k, (q // 4) % 2, q % 4)

    def along(q):
        return device(xh, q // 2, q % 2, xl, y)

    def group(q):
        return device(q // 8, q % 8, k, xl, y)

    def row_of(q):
        return device(xh, z, k, q // 4, q % 4)

    owner = [co[p] // 2 for p in range(2)]
    local = [co[p] % 2 for p in range(2)]
    o_xh = [o // 16 for o in owner]
    o_z = [(o // 2) % 8 for o in owner]
    o_k = [o % 2 for o in owner]

    barrier = pltpu.get_barrier_semaphore()

    def greet(count, skip, target):
        def step(q, carry):
            @pl.when(jnp.logical_not(skip(q)))
            def _():
                pl.semaphore_signal(barrier, inc=1, device_id=target(q), device_id_type=MESH)

            return carry

        lax.fori_loop(0, count, step, 0)

    greet(16, lambda q: q == me_plane, plane)
    greet(16, lambda q: q == me_zk, along)
    greet(8, lambda q: q == z, lambda q: device(1 - xh, q, k, xl, y))
    pl.semaphore_wait(barrier, 37)

    lead = ((0, 0), (0, 1), (1, 1))
    for t, (p, n) in enumerate(lead):
        tile = mat[local[p], ro[n] % 8]
        for q in range(16):
            dst1[q, t] = tile[8 * q : 8 * q + 8, :]
    rd1[me_plane] = dst1[me_plane]
    d1_args = (16, me_plane, lambda q: dst1.at[q], lambda q: rd1.at[q], plane, d1, e1)
    send_all(*d1_args)

    for p in range(2):
        st1[p] = mat[local[p], pl.ds(4 * (1 - k), 4)]
    sib = device(xh, z, 1 - k, xl, y)
    split = pltpu.make_async_remote_copy(
        src_ref=st1, dst_ref=rc1, send_sem=s1, recv_sem=r1, device_id=sib, device_id_type=MESH
    )
    split.start()

    recv_all(*d1_args)
    for t, (p, n) in enumerate(lead):
        slot = ro[n] // 8
        pd1[t] = rd1[(o_xh[p] * 2 + slot // 4) * 4 + slot % 4, t]
    rd2[me_zk] = pd1[...]
    d2_args = (16, me_zk, lambda q: pd1, lambda q: rd2.at[q], along, d2, e2)
    send_all(*d2_args)
    split.wait()
    for p in range(2):
        mine = mat[local[p], pl.ds(4 * k, 4)]
        half[pl.ds(4 * p, 4)] = jnp.where(o_k[p] == k, mine, rc1[p])
    recv_all(*d2_args)
    for t, (p, n) in enumerate(lead):
        pd2[t] = rd2[o_z[p] * 2 + o_k[p], t]
    diag[me_plane] = pd2[...]
    d3_args = (16, me_plane, lambda q: pd2, lambda q: diag.at[q], plane, d3, e3)
    send_all(*d3_args)

    rc2[me_xz] = half[z, pl.ds(64 * xh, 64), :]
    r2_args = (
        16, me_xz, lambda q: half.at[q % 8, pl.ds(64 * (q // 8), 64), :],
        lambda q: rc2.at[q], group, s2, r2,
    )
    send_all(*r2_args)
    recv_all(*d3_args)
    recv_all(*r2_args)
    src = jnp.where(z < 4, o_xh[0] * 8 + o_z[0], o_xh[1] * 8 + o_z[1])
    piece = rc2[src]
    pc2[...] = piece

    def rows_slot(q):
        zz = q % 8
        return rows.at[zz // 4, 4 * k + zz % 4, pl.ds(64 * (q // 8), 64), :]

    rows[z // 4, 4 * k + z % 4, pl.ds(64 * xh, 64), :] = piece
    r4_args = (16, me_xz, lambda q: pc2, rows_slot, group, s4, r4)
    send_all(*r4_args)
    base = 2 * ((xh * 8 + z) * 2 + k)

    def find(n, carry):
        c = co[n]
        s = ro[n]
        return (
            carry[0] + jnp.where(c == base, s, 0),
            carry[1] + jnp.where(c == base + 1, s, 0),
        )

    slots = lax.fori_loop(0, NODES, find, (jnp.int32(0), jnp.int32(0)))
    recv_all(*r4_args)

    def join(p):
        mine = rows.at[p, pl.ds(4 * k, 4)]
        return pltpu.make_async_remote_copy(
            src_ref=mine, dst_ref=mine, send_sem=s5.at[p], recv_sem=r5.at[p],
            device_id=sib, device_id_type=MESH,
        )

    def joined(p):
        return pltpu.make_async_remote_copy(
            src_ref=rows.at[p, pl.ds(4 * k, 4)],
            dst_ref=rows.at[p, pl.ds(4 * (1 - k), 4)],
            send_sem=s5.at[p], recv_sem=r5.at[p], device_id=sib, device_id_type=MESH,
        )

    for p in range(2):
        join(p).start()
    for p in range(2):
        copy = joined(p)
        copy.wait_send()
        copy.wait_recv()

    for p in range(2):
        for l in range(2):
            tile = rows[p, slots[l] % 8]
            cst[4 * p + 2 * l] = tile[:64]
            cst[4 * p + 2 * l + 1] = tile[64:]
    rc3[me_row] = cst[me_row]
    c1_args = (8, me_row, lambda q: cst.at[q], lambda q: rc3.at[q], row_of, s6, r6)
    send_all(*c1_args)
    recv_all(*c1_args)
    from_row = jnp.where((me_row // 2) % 2 == 0, slots[0] // 8, slots[1] // 8)
    piece = rc3[from_row]
    pc3[...] = piece
    cols[me_row] = piece
    c2_args = (8, me_row, lambda q: pc3, lambda q: cols.at[q], row_of, s7, r7)
    send_all(*c2_args)
    recv_all(*c2_args)

    rows_out[...] = rows[...]
    cols_out[...] = cols[...]
    diag_out[...] = diag[...]


def gather_tiles(mat, co, ro):
    vmem = pl.BlockSpec(memory_space=pltpu.VMEM)
    smem = pl.BlockSpec(memory_space=pltpu.SMEM)
    dma = pltpu.SemaphoreType.DMA
    return pl.pallas_call(
        comm_kernel,
        out_shape=(
            jax.ShapeDtypeStruct((2, 8, W, W), F32),
            jax.ShapeDtypeStruct((8, 64, W), F32),
            jax.ShapeDtypeStruct((16, 3, 8, W), F32),
        ),
        in_specs=[vmem, smem, smem],
        out_specs=(vmem, vmem, vmem),
        scratch_shapes=[
            pltpu.VMEM((2, 4, W, W), F32),
            pltpu.VMEM((2, 4, W, W), F32),
            pltpu.VMEM((8, W, W), F32),
            pltpu.VMEM((16, 64, W), F32),
            pltpu.VMEM((64, W), F32),
            pltpu.VMEM((2, 8, W, W), F32),
            pltpu.VMEM((8, 64, W), F32),
            pltpu.VMEM((8, 64, W), F32),
            pltpu.VMEM((64, W), F32),
            pltpu.VMEM((8, 64, W), F32),
            pltpu.VMEM((16, 3, 8, W), F32),
            pltpu.VMEM((16, 3, 8, W), F32),
            pltpu.VMEM((3, 8, W), F32),
            pltpu.VMEM((16, 3, 8, W), F32),
            pltpu.VMEM((3, 8, W), F32),
            pltpu.VMEM((16, 3, 8, W), F32),
            dma, dma,
            dma((16,)), dma((16,)),
            dma((16,)), dma((16,)),
            dma((2,)), dma((2,)),
            dma((8,)), dma((8,)),
            dma((8,)), dma((8,)),
            dma((16,)), dma((16,)),
            dma((16,)), dma((16,)),
            dma((16,)), dma((16,)),
        ],
        compiler_params=pltpu.CompilerParams(
            collective_id=0, has_side_effects=True, vmem_limit_bytes=32 * 1024 * 1024
        ),
        name="gather_tiles",
    )(mat, co, ro)


def lanes(x):
    return jnp.broadcast_to(x, (x.shape[0], W))


def subs(x):
    return jnp.broadcast_to(x, (8, W))


def factor(wa_ref, wb_ref):
    rid = lax.broadcasted_iota(jnp.int32, (8, W), 0)
    for c in range(0, W, 8):
        wa = wa_ref[c : c + 8, :]
        wb = wb_ref[c : c + 8, :]
        cl = [lanes(wa[:, c + i : c + i + 1]) for i in range(8)]
        pa, pb, sc, lt = [], [], [], []
        for i in range(8):
            s = lax.rsqrt(subs(cl[i][i : i + 1]))
            li = cl[i] * s
            ra = subs(wa[i : i + 1]) * s
            rb = subs(wb[i : i + 1]) * s
            low = jnp.where(rid > i, li, 0.0)
            wa = jnp.where(rid == i, ra, wa - low * ra)
            wb = jnp.where(rid == i, rb, wb - low * rb)
            row = {}
            for j in range(i + 1, 8):
                row[j] = subs(li[j : j + 1])
                cl[j] = cl[j] - li * row[j]
            pa.append(ra)
            pb.append(rb)
            sc.append(s)
            lt.append(row)
        wa_ref[c : c + 8, :] = wa
        wb_ref[c : c + 8, :] = wb
        g = c + 8
        while g < W:
            size = min(16, W - g)
            tile = lambda v: jnp.concatenate([v] * (size // 8), axis=0) if size > 8 else v
            ga = wa_ref[g : g + size, :]
            gb = wb_ref[g : g + size, :]
            gc = [lanes(ga[:, c + i : c + i + 1]) for i in range(8)]
            for i in range(8):
                li = gc[i] * tile(sc[i])
                ga = ga - li * tile(pa[i])
                gb = gb - li * tile(pb[i])
                for j in range(i + 1, 8):
                    gc[j] = gc[j] - li * tile(lt[i][j])
            wa_ref[g : g + size, :] = ga
            wb_ref[g : g + size, :] = gb
            g += size


def nt(a, b):
    return lax.dot_general(a, b, (((1,), (1,)), ((), ())), precision=PRECISE, preferred_element_type=F32)


def apply_kernel(mat, rows, cols, diag, co, ro, pat, out, wa, wb, f0, f1, g0, g1, inv_row, inv_col):
    col = lax.axis_index("col")
    row = lax.axis_index("row")

    def invert(n, carry):
        inv_row[ro[n]] = n
        inv_col[co[n]] = n
        return carry

    lax.fori_loop(0, NODES, invert, 0)
    row_node = [inv_row[8 * row + s] for s in range(8)]
    col_node = [inv_col[2 * col + l] for l in range(2)]
    rid = lax.broadcasted_iota(jnp.int32, (W, W), 0)
    cid = lax.broadcasted_iota(jnp.int32, (W, W), 1)
    eye = jnp.where(rid == cid, 1.0, 0.0).astype(F32)

    def lead(t):
        return jnp.concatenate([diag[q, t] for q in range(16)], axis=0)

    def col_tile(p, l):
        return jnp.concatenate([cols[4 * p + 2 * l], cols[4 * p + 2 * l + 1]], axis=0)

    def finish(l, s, value):
        out[l, s] = value

    wa[...] = lead(0)
    wb[...] = eye
    factor(wa, wb)
    lower0 = jnp.where(rid <= cid, wa[...], 0.0).T
    inv0 = wb[...]
    f01 = nt(lead(1), inv0)
    a11 = lead(2) - nt(f01, f01)
    for s in range(8):
        keep = pat[0, row_node[s]] == 1
        f0[s] = jnp.where(keep, nt(rows[0, s], inv0), 0.0)
    for l in range(2):
        keep = pat[0, col_node[l]] == 1
        g0[l] = jnp.where(keep, nt(col_tile(0, l), inv0), 0.0)
    wa[...] = a11
    wb[...] = eye
    factor(wa, wb)
    lower1 = jnp.where(rid <= cid, wa[...], 0.0).T
    inv1 = wb[...]
    for s in range(8):
        keep = pat[1, row_node[s]] == 1
        f1[s] = jnp.where(keep, nt(rows[1, s] - nt(f0[s], f01), inv1), 0.0)
    for l in range(2):
        keep = pat[1, col_node[l]] == 1
        g1[l] = jnp.where(keep, nt(col_tile(1, l) - nt(g0[l], f01), inv1), 0.0)
    for l in range(2):
        for s in range(8):
            old = mat[l, s]
            new = old - nt(f0[s], g0[l]) - nt(f1[s], g1[l])
            new = jnp.where(row_node[s] >= col_node[l], new, old)
            for p, (f, low) in enumerate(((f0, lower0), (f1, lower1))):
                here = col_node[l] == p
                new = jnp.where(here & (pat[p, row_node[s]] == 1), f[s], new)
                new = jnp.where(here & (row_node[s] == p), low, new)
            out[l, s] = new


def apply_panels(mat, rows, cols, diag, co, ro, pat):
    vmem = pl.BlockSpec(memory_space=pltpu.VMEM)
    smem = pl.BlockSpec(memory_space=pltpu.SMEM)
    return pl.pallas_call(
        apply_kernel,
        out_shape=jax.ShapeDtypeStruct((2, 8, W, W), F32),
        in_specs=[vmem] * 4 + [smem] * 3,
        out_specs=vmem,
        scratch_shapes=[
            pltpu.VMEM((W, W), F32),
            pltpu.VMEM((W, W), F32),
            pltpu.VMEM((8, W, W), F32),
            pltpu.VMEM((8, W, W), F32),
            pltpu.VMEM((2, W, W), F32),
            pltpu.VMEM((2, W, W), F32),
            pltpu.SMEM((NODES,), jnp.int32),
            pltpu.SMEM((NODES,), jnp.int32),
        ],
        compiler_params=pltpu.CompilerParams(vmem_limit_bytes=32 * 1024 * 1024),
        name="apply_panels",
    )(mat, rows, cols, diag, co, ro, pat)


def body(matrix, col_owner, row_owner, pattern):
    rows, cols, diag = gather_tiles(matrix, col_owner, row_owner)
    return apply_panels(matrix, rows, cols, diag, col_owner, row_owner, pattern)


def solution(mesh):
    return jax.shard_map(
        body,
        mesh=mesh,
        in_specs=(P("col", "row", None, None), P(), P(), P()),
        out_specs=P("col", "row", None, None),
        check_vma=False,
    )
```

time: 761 us -> 85.9 us (0.11)
  the two profiles are of different devices: /device:TPU:1 before, /device:TPU:71 now
where the time goes in v1:
time: 85.9 us; the launch traced here: 85.8 us
  Pallas kernels  82.6 us (96%)
  local copies, waits for them, and re-layouts  3.21 us (4%)
    pallas_call x1, Pallas kernels, gather_tiles(): pl.pallas_call(comm_kernel, out_shape=(jax.ShapeDtypeStruct((2, 8, W, W),...  65.5 us
    pallas_call x1, Pallas kernels, apply_panels(): pl.pallas_call(apply_kernel, out_shape=jax.ShapeDtypeStruct((2, 8, W, W),...  17 us
    unnamed x8, local copies, waits for them, and re-layouts  3.21 us

profile of v1, /device:TPU:71, one launch (start us, length us, event | category | flops | bytes accessed | tf_op | source)
XLA Modules:
  0.0 85.8 jit_solution(9831382725048280575)
XLA Ops:
  0.0 0.0 copy-start
  0.0 1.2 %copy-done = f32[2,8,128,128]{3,2,1,0:T(8,128)S(1)} copy-done((f32[2,8,128,128]{3,2,1,0:T(8,128)S(1)}, f32[2,8,128,128]{3,2,1,0:T(8,128)}, u32[]{:S(2)}) %copy-start) | copy-done | bytes 1048600
  1.2 0.0 copy-start.1
  1.2 0.7 copy-done.1
  1.9 0.0 copy-start.2
  1.9 0.7 copy-done.2
  2.5 65.5 %gather_tiles.1 = (f32[2,8,128,128]{3,2,1,0:T(8,128)S(1)}, f32[8,64,128]{2,1,0:T(8,128)S(1)}, f32[16,3,8,128]{3,2,1,0:T(8,128)S(1)}) custom-call(f32[2,8,128,128]{3,2,1,0:T(8,128)S(1)} %copy-done, s32[64]{0:T(128)S(1)} %copy-done.1, s32[64]{0:T(128)S(1)} %copy-done.2), custom_call_target="tpu_custom_call" | custom-call | tf_op jit(solution)/shard_map/gather_tiles/pallas_call | solution.py:226
  68.1 0.0 copy-start.3
  68.1 0.7 copy-done.3
  68.8 17.0 %apply_panels.1 = f32[2,8,128,128]{3,2,1,0:T(8,128)} custom-call(f32[2,8,128,128]{3,2,1,0:T(8,128)S(1)} %copy-done, f32[2,8,128,128]{3,2,1,0:T(8,128)S(1)} %get-tuple-element.8.rows, f32[8,64,128]{2,1,0:T(8,128)S(1)} %get-tuple-element.9.cols, f32[16,3,8,128]{3,2,1,0:T(8,128)S(1)} %get-tuple-element.10.diag, s32[64]{0:T(128)S(1)} %copy-done.1, ...), custom_call_target="tpu_custom_call" | custom-call | tf_op jit(solution)/shard_map/apply_panels/pallas_call | solution.py:388
Async XLA Ops:
  0.0 1.2 %copy-start = (f32[2,8,128,128]{3,2,1,0:T(8,128)S(1)}, f32[2,8,128,128]{3,2,1,0:T(8,128)}, u32[]{:S(2)}) copy-start(f32[2,8,128,128]{3,2,1,0:T(8,128)} %mat.3) | copy-start | bytes 3145732
  1.2 0.7 copy-start.1
  1.9 0.7 copy-start.2
  68.1 0.7 copy-start.3

commit v2 on v1

v2 whole, which is shorter than its diff:
```python
import functools

import jax
import jax.numpy as jnp
from jax import lax
from jax.experimental import pallas as pl
from jax.experimental.pallas import tpu as pltpu
from jax.sharding import PartitionSpec as P

MESH = pl.DeviceIdType.MESH
F32 = jnp.float32
PRECISE = lax.Precision.HIGHEST
W = 128
NODES = 64


def my_place():
    col = lax.axis_index("col")
    row = lax.axis_index("row")
    return col // 16, (col // 2) % 8, col % 2, row // 4, row % 4


def device(xh, z, k, xl, y):
    return {"col": (xh * 8 + z) * 2 + k, "row": xl * 4 + y}


def send_all(count, me, source, slot, target, send_sem, recv_sem):
    def step(q, carry):
        @pl.when(q != me)
        def _():
            pltpu.make_async_remote_copy(
                src_ref=source(q),
                dst_ref=slot(me),
                send_sem=send_sem.at[q],
                recv_sem=recv_sem.at[me],
                device_id=target(q),
                device_id_type=MESH,
            ).start()

        return carry

    lax.fori_loop(0, count, step, 0)


def recv_all(count, me, source, slot, target, send_sem, recv_sem):
    def step(q, carry):
        @pl.when(q != me)
        def _():
            copy = pltpu.make_async_remote_copy(
                src_ref=source(q),
                dst_ref=slot(q),
                send_sem=send_sem.at[q],
                recv_sem=recv_sem.at[q],
                device_id=target(q),
                device_id_type=MESH,
            )
            copy.wait_send()
            copy.wait_recv()

        return carry

    lax.fori_loop(0, count, step, 0)


def place_lead(diag, t, dst):
    for k in range(2):
        for q in range(16):
            dst[64 * k + 4 * q : 64 * k + 4 * q + 4, :] = diag[k, q, t]


def comm_kernel(
    mat_hbm, co_hbm, ro_hbm, rows_out, cols_out, inv_out, low_out, f01_out,
    mat, co, ro, st1, rc1, stl, rcl, half, leadh, rc2, pc2, rows, cst, rc3, pc3, cols,
    dst1, rd1, pd1, rd2, diag, wa, wb, tile_a,
    ld, s1, r1, s2, r2, s4, r4, s5, r5, s6, r6, s7, r7, d1, e1, d2, e2, d3, e3, d4, e4,
):
    xh, z, k, xl, y = my_place()
    me_plane = (xh * 2 + xl) * 4 + y
    me_xz = xh * 8 + z
    me_row = xl * 4 + y

    def plane(q):
        return device(q // 8, z, k, (q // 4) % 2, q % 4)

    def along(q):
        return device(xh, q, k, xl, y)

    def group(q):
        return device(q // 8, q % 8, k, xl, y)

    def row_of(q):
        return device(xh, z, k, q // 4, q % 4)

    sib = device(xh, z, 1 - k, xl, y)
    loads = [
        pltpu.make_async_copy(co_hbm, co, ld.at[0]),
        pltpu.make_async_copy(ro_hbm, ro, ld.at[1]),
        pltpu.make_async_copy(mat_hbm, mat, ld.at[2]),
    ]
    for copy in loads:
        copy.start()

    barrier = pltpu.get_barrier_semaphore()

    def greet(count, me, target):
        def step(q, carry):
            @pl.when(q != me)
            def _():
                pl.semaphore_signal(barrier, inc=1, device_id=target(q), device_id_type=MESH)

            return carry

        lax.fori_loop(0, count, step, 0)

    greet(16, me_xz, group)
    greet(8, me_row, row_of)

    def far(q, carry):
        @pl.when(q != me_row)
        def _():
            pl.semaphore_signal(
                barrier, inc=1, device_id=device(1 - xh, z, k, q // 4, q % 4), device_id_type=MESH
            )

        return carry

    lax.fori_loop(0, 8, far, 0)
    pl.semaphore_signal(barrier, inc=1, device_id=sib, device_id_type=MESH)
    for copy in loads:
        copy.wait()

    owner = [co[p] // 2 for p in range(2)]
    local = [co[p] % 2 for p in range(2)]
    o_xh = [o // 16 for o in owner]
    o_z = [(o // 2) % 8 for o in owner]
    o_k = [o % 2 for o in owner]
    lead = ((0, 0), (0, 1), (1, 1))
    for p in range(2):
        st1[p] = mat[local[p], pl.ds(4 * (1 - k), 4)]
    for t, (p, n) in enumerate(lead):
        stl[t] = mat[local[p], ro[n] % 8, pl.ds(64 * (1 - k), 64), :]
    pl.semaphore_wait(barrier, 15 + 7 + 7 + 1)

    def to_sibling(src, dst, send, recv):
        return pltpu.make_async_remote_copy(
            src_ref=src, dst_ref=dst, send_sem=send, recv_sem=recv, device_id=sib, device_id_type=MESH
        )

    split_lead = to_sibling(stl, rcl, s1.at[0], r1.at[0])
    split_half = to_sibling(st1, rc1, s1.at[1], r1.at[1])
    split_lead.start()
    split_half.start()
    split_lead.wait()
    for t, (p, n) in enumerate(lead):
        mine = mat[local[p], ro[n] % 8, pl.ds(64 * k, 64), :]
        leadh[t] = jnp.where(o_k[p] == k, mine, rcl[t])
        for q in range(16):
            dst1[q, t] = leadh[t, 4 * q : 4 * q + 4, :]
    rd1[me_plane] = dst1[me_plane]
    d1_args = (16, me_plane, lambda q: dst1.at[q], lambda q: rd1.at[q], plane, d1, e1)
    send_all(*d1_args)
    split_half.wait()
    for p in range(2):
        mine = mat[local[p], pl.ds(4 * k, 4)]
        half[pl.ds(4 * p, 4)] = jnp.where(o_k[p] == k, mine, rc1[p])

    rc2[me_xz] = half[z, pl.ds(64 * xh, 64), :]
    r2_args = (
        16, me_xz, lambda q: half.at[q % 8, pl.ds(64 * (q // 8), 64), :],
        lambda q: rc2.at[q], group, s2, r2,
    )
    send_all(*r2_args)

    recv_all(*d1_args)
    for t, (p, n) in enumerate(lead):
        slot = ro[n] // 8
        pd1[t] = rd1[(o_xh[p] * 2 + slot // 4) * 4 + slot % 4, t]
    rd2[z] = pd1[...]
    d2_args = (8, z, lambda q: pd1, lambda q: rd2.at[q], along, d2, e2)
    send_all(*d2_args)
    recv_all(*d2_args)
    for t, (p, n) in enumerate(lead):
        diag[k, me_plane, t] = rd2[o_z[p], t]
    d3_args = (16, me_plane, lambda q: diag.at[k, me_plane], lambda q: diag.at[k, q], plane, d3, e3)
    send_all(*d3_args)

    recv_all(*r2_args)
    src = jnp.where(z < 4, o_xh[0] * 8 + o_z[0], o_xh[1] * 8 + o_z[1])
    piece = rc2[src]
    pc2[...] = piece

    def rows_slot(q):
        zz = q % 8
        return rows.at[zz // 4, 4 * k + zz % 4, pl.ds(64 * (q // 8), 64), :]

    rows[z // 4, 4 * k + z % 4, pl.ds(64 * xh, 64), :] = piece
    r4_args = (16, me_xz, lambda q: pc2, rows_slot, group, s4, r4)
    send_all(*r4_args)

    recv_all(*d3_args)
    to_sibling(diag.at[k], diag.at[k], d4, e4).start()
    base = 2 * ((xh * 8 + z) * 2 + k)

    def find(n, carry):
        c = co[n]
        s = ro[n]
        return (
            carry[0] + jnp.where(c == base, s, 0),
            carry[1] + jnp.where(c == base + 1, s, 0),
        )

    slots = lax.fori_loop(0, NODES, find, (jnp.int32(0), jnp.int32(0)))
    joined_lead = to_sibling(diag.at[k], diag.at[1 - k], d4, e4)
    joined_lead.wait_send()
    joined_lead.wait_recv()

    rid = lax.broadcasted_iota(jnp.int32, (W, W), 0)
    cid = lax.broadcasted_iota(jnp.int32, (W, W), 1)
    eye = jnp.where(rid == cid, 1.0, 0.0).astype(F32)
    place_lead(diag, 0, wa)
    wb[...] = eye
    factor(wa, wb)
    low_out[0] = jnp.where(rid <= cid, wa[...], 0.0).T
    inv0 = wb[...]
    inv_out[0] = inv0
    place_lead(diag, 1, tile_a)
    f01 = nt(tile_a[...], inv0)
    f01_out[...] = f01
    place_lead(diag, 2, wa)
    wa[...] = wa[...] - nt(f01, f01)
    wb[...] = eye
    factor(wa, wb)
    low_out[1] = jnp.where(rid <= cid, wa[...], 0.0).T
    inv_out[1] = wb[...]

    recv_all(*r4_args)
    for p in range(2):
        mine = rows.at[p, pl.ds(4 * k, 4)]
        to_sibling(mine, mine, s5.at[p], r5.at[p]).start()
    for p in range(2):
        copy = to_sibling(
            rows.at[p, pl.ds(4 * k, 4)], rows.at[p, pl.ds(4 * (1 - k), 4)], s5.at[p], r5.at[p]
        )
        copy.wait_send()
        copy.wait_recv()

    for p in range(2):
        for l in range(2):
            tile = rows[p, slots[l] % 8]
            cst[4 * p + 2 * l] = tile[:64]
            cst[4 * p + 2 * l + 1] = tile[64:]
    rc3[me_row] = cst[me_row]
    c1_args = (8, me_row, lambda q: cst.at[q], lambda q: rc3.at[q], row_of, s6, r6)
    send_all(*c1_args)
    recv_all(*c1_args)
    from_row = jnp.where((me_row // 2) % 2 == 0, slots[0] // 8, slots[1] // 8)
    piece = rc3[from_row]
    pc3[...] = piece
    cols[me_row] = piece
    c2_args = (8, me_row, lambda q: pc3, lambda q: cols.at[q], row_of, s7, r7)
    send_all(*c2_args)
    rows_out[...] = rows[...]
    recv_all(*c2_args)
    cols_out[...] = cols[...]


def gather_tiles(mat, co, ro):
    vmem = pl.BlockSpec(memory_space=pltpu.VMEM)
    hbm = pl.BlockSpec(memory_space=pltpu.HBM)
    dma = pltpu.SemaphoreType.DMA
    vm = lambda *shape: pltpu.VMEM(shape, F32)
    pair = lambda n: [dma((n,)), dma((n,))]
    return pl.pallas_call(
        comm_kernel,
        out_shape=(
            jax.ShapeDtypeStruct((2, 8, W, W), F32),
            jax.ShapeDtypeStruct((8, 64, W), F32),
            jax.ShapeDtypeStruct((2, W, W), F32),
            jax.ShapeDtypeStruct((2, W, W), F32),
            jax.ShapeDtypeStruct((W, W), F32),
        ),
        in_specs=[hbm, hbm, hbm],
        out_specs=(vmem,) * 5,
        scratch_shapes=[
            vm(2, 8, W, W),
            pltpu.SMEM((NODES,), jnp.int32),
            pltpu.SMEM((NODES,), jnp.int32),
            vm(2, 4, W, W), vm(2, 4, W, W),
            vm(3, 64, W), vm(3, 64, W),
            vm(8, W, W), vm(3, 64, W),
            vm(16, 64, W), vm(64, W), vm(2, 8, W, W),
            vm(8, 64, W), vm(8, 64, W), vm(64, W), vm(8, 64, W),
            vm(16, 3, 4, W), vm(16, 3, 4, W), vm(3, 4, W), vm(8, 3, 4, W), vm(2, 16, 3, 4, W),
            vm(W, W), vm(W, W), vm(W, W),
            dma((3,)),
            *pair(2), *pair(16), *pair(16), *pair(2), *pair(8), *pair(8),
            *pair(16), *pair(8), *pair(16), dma, dma,
        ],
        compiler_params=pltpu.CompilerParams(
            collective_id=0, has_side_effects=True, vmem_limit_bytes=32 * 1024 * 1024
        ),
        name="gather_tiles",
    )(mat, co, ro)


def lanes(x):
    return jnp.broadcast_to(x, (x.shape[0], W))


def subs(x):
    return jnp.broadcast_to(x, (8, W))


def factor(wa_ref, wb_ref):
    rid = lax.broadcasted_iota(jnp.int32, (8, W), 0)
    for c in range(0, W, 8):
        wa = wa_ref[c : c + 8, :]
        wb = wb_ref[c : c + 8, :]
        cl = [lanes(wa[:, c + i : c + i + 1]) for i in range(8)]
        pa, pb, sc, lt = [], [], [], []
        for i in range(8):
            s = lax.rsqrt(subs(cl[i][i : i + 1]))
            li = cl[i] * s
            ra = subs(wa[i : i + 1]) * s
            rb = subs(wb[i : i + 1]) * s
            low = jnp.where(rid > i, li, 0.0)
            wa = jnp.where(rid == i, ra, wa - low * ra)
            wb = jnp.where(rid == i, rb, wb - low * rb)
            row = {}
            for j in range(i + 1, 8):
                row[j] = subs(li[j : j + 1])
                cl[j] = cl[j] - li * row[j]
            pa.append(ra)
            pb.append(rb)
            sc.append(s)
            lt.append(row)
        wa_ref[c : c + 8, :] = wa
        wb_ref[c : c + 8, :] = wb
        g = c + 8
        while g < W:
            size = min(16, W - g)
            tile = lambda v: jnp.concatenate([v] * (size // 8), axis=0) if size > 8 else v
            ga = wa_ref[g : g + size, :]
            gb = wb_ref[g : g + size, :]
            gc = [lanes(ga[:, c + i : c + i + 1]) for i in range(8)]
            for i in range(8):
                li = gc[i] * tile(sc[i])
                ga = ga - li * tile(pa[i])
                gb = gb - li * tile(pb[i])
                for j in range(i + 1, 8):
                    gc[j] = gc[j] - li * tile(lt[i][j])
            wa_ref[g : g + size, :] = ga
            wb_ref[g : g + size, :] = gb
            g += size


def nt(a, b):
    return lax.dot_general(a, b, (((1,), (1,)), ((), ())), precision=PRECISE, preferred_element_type=F32)


def nt16(a, b):
    return lax.dot_general(a, b, (((1,), (1,)), ((), ())), preferred_element_type=F32)


def parts(a):
    high = a.astype(jnp.bfloat16)
    return high, (a - high.astype(F32)).astype(jnp.bfloat16)


def nt3(a, b):
    ah, al = parts(a)
    bh, bl = parts(b)
    both = nt16(jnp.concatenate([ah, al], axis=1), jnp.concatenate([bh, bh], axis=1))
    return both + nt16(ah, bl)


def apply_kernel(mat, rows, cols, inv, low, f01, co, ro, pat, out, f0, f1, g0, g1, inv_row, inv_col):
    col = lax.axis_index("col")
    row = lax.axis_index("row")

    def invert(n, carry):
        inv_row[ro[n]] = n
        inv_col[co[n]] = n
        return carry

    lax.fori_loop(0, NODES, invert, 0)
    row_node = [inv_row[8 * row + s] for s in range(8)]
    col_node = [inv_col[2 * col + l] for l in range(2)]
    keep_row = [[pat[p, row_node[s]] == 1 for s in range(8)] for p in range(2)]
    keep_col = [[pat[p, col_node[l]] == 1 for l in range(2)] for p in range(2)]

    def mask(value, keeps):
        return jnp.concatenate(
            [jnp.where(keep, value[W * i : W * i + W], 0.0) for i, keep in enumerate(keeps)], axis=0
        )

    raw = lambda p: cols[4 * p : 4 * p + 4].reshape(2 * W, W)
    f0[...] = mask(nt3(rows[0].reshape(8 * W, W), inv[0]), keep_row[0])
    g0[...] = mask(nt3(raw(0), inv[0]), keep_col[0])
    f1[...] = mask(
        nt3(rows[1].reshape(8 * W, W) - nt3(f0[...], f01[...]), inv[1]), keep_row[1]
    )
    g1[...] = mask(nt3(raw(1) - nt3(g0[...], f01[...]), inv[1]), keep_col[1])
    g0h, g0l = parts(g0[...])
    g1h, g1l = parts(g1[...])
    gh = jnp.concatenate([g0h, g1h], axis=1)
    gl = jnp.concatenate([g0l, g1l], axis=1)
    for s in range(8):
        rows_s = slice(W * s, W * s + W)
        f0h, f0l = parts(f0[rows_s])
        f1h, f1l = parts(f1[rows_s])
        fh = jnp.concatenate([f0h, f1h], axis=1)
        fl = jnp.concatenate([f0l, f1l], axis=1)
        step = nt16(fh, gh) + nt16(fl, gh) + nt16(fh, gl)
        for l in range(2):
            old = mat[l, s]
            new = jnp.where(row_node[s] >= col_node[l], old - step[:, W * l : W * l + W], old)
            for p, f in enumerate((f0, f1)):
                here = col_node[l] == p
                new = jnp.where(here & keep_row[p][s], f[rows_s], new)
                new = jnp.where(here & (row_node[s] == p), low[p], new)
            out[l, s] = new


def apply_panels(mat, rows, cols, inv, low, f01, co, ro, pat):
    vmem = pl.BlockSpec(memory_space=pltpu.VMEM)
    smem = pl.BlockSpec(memory_space=pltpu.SMEM)
    return pl.pallas_call(
        apply_kernel,
        out_shape=jax.ShapeDtypeStruct((2, 8, W, W), F32),
        in_specs=[vmem] * 6 + [smem] * 3,
        out_specs=vmem,
        scratch_shapes=[
            pltpu.VMEM((8 * W, W), F32),
            pltpu.VMEM((8 * W, W), F32),
            pltpu.VMEM((2 * W, W), F32),
            pltpu.VMEM((2 * W, W), F32),
            pltpu.SMEM((NODES,), jnp.int32),
            pltpu.SMEM((NODES,), jnp.int32),
        ],
        compiler_params=pltpu.CompilerParams(vmem_limit_bytes=32 * 1024 * 1024),
        name="apply_panels",
    )(mat, rows, cols, inv, low, f01, co, ro, pat)


def body(matrix, col_owner, row_owner, pattern):
    found = gather_tiles(matrix, col_owner, row_owner)
    return apply_panels(matrix, *found, col_owner, row_owner, pattern)


def solution(mesh):
    return jax.shard_map(
        body,
        mesh=mesh,
        in_specs=(P("col", "row", None, None), P(), P(), P()),
        out_specs=P("col", "row", None, None),
        check_vma=False,
    )
```

time: 85.9 us -> 64 us (0.75)
  the two profiles are of different devices: /device:TPU:71 before, /device:TPU:1 now
where the time goes in v2:
time: 64 us; the launch traced here: 63.4 us
  Pallas kernels  60.2 us (94%)
  local copies, waits for them, and re-layouts  3.21 us (5%)
    pallas_call x1, Pallas kernels, gather_tiles(): pl.pallas_call(comm_kernel, out_shape=(jax.ShapeDtypeStruct((2, 8, W, W),...  55.8 us
    pallas_call x1, Pallas kernels, apply_panels(): pl.pallas_call(apply_kernel, out_shape=jax.ShapeDtypeStruct((2, 8, W, W),...  4.4 us
    unnamed x8, local copies, waits for them, and re-layouts  3.21 us

profile of v2, /device:TPU:1, one launch (start us, length us, event | category | flops | bytes accessed | tf_op | source)
XLA Modules:
  0.0 63.4 jit_solution(12631403755272711772)
XLA Ops:
  0.0 0.0 copy-start
  0.0 1.2 %copy-done = f32[2,8,128,128]{3,2,1,0:T(8,128)S(1)} copy-done((f32[2,8,128,128]{3,2,1,0:T(8,128)S(1)}, f32[2,8,128,128]{3,2,1,0:T(8,128)}, u32[]{:S(2)}) %copy-start) | copy-done | bytes 1048600
  1.2 0.0 copy-start.1
  1.2 0.7 %copy-done.1 = s32[64]{0:T(128)S(1)} copy-done((s32[64]{0:T(128)S(1)}, s32[64]{0:T(128)}, u32[]{:S(2)}) %copy-start.1) | copy-done | bytes 280
  1.9 0.0 copy-start.2
  1.9 0.7 %copy-done.2 = s32[64]{0:T(128)S(1)} copy-done((s32[64]{0:T(128)S(1)}, s32[64]{0:T(128)}, u32[]{:S(2)}) %copy-start.2) | copy-done | bytes 280
  2.5 55.8 %gather_tiles.1 = (f32[2,8,128,128]{3,2,1,0:T(8,128)S(1)}, f32[8,64,128]{2,1,0:T(8,128)S(1)}, f32[2,128,128]{2,1,0:T(8,128)S(1)}, f32[2,128,128]{2,1,0:T(8,128)S(1)}, f32[128,128]{1,0:T(8,128)S(1)}) custom-call(f32[2,8,128,128]{3,2,1,0:T(8,128)S(1)} %copy-done, s32[64]{0:T(128)S(1)} %copy-done.1, s32[64]{0:T(128)S(1)} %copy-done.2), custom_call_target="tpu_custom_call" | custom-call | tf_op jit(solution)/shard_map/gather_tiles/pallas_call | solution.py:273
  58.3 0.0 copy-start.3
  58.3 0.7 %copy-done.3 = s32[2,64]{1,0:T(2,128)S(1)} copy-done((s32[2,64]{1,0:T(2,128)S(1)}, s32[2,64]{1,0:T(2,128)}, u32[]{:S(2)}) %copy-start.3) | copy-done | bytes 536
  59.0 4.4 %apply_panels.1 = f32[2,8,128,128]{3,2,1,0:T(8,128)} custom-call(f32[2,8,128,128]{3,2,1,0:T(8,128)S(1)} %copy-done, f32[2,8,128,128]{3,2,1,0:T(8,128)S(1)} %get-tuple-element.10.rows, f32[8,64,128]{2,1,0:T(8,128)S(1)} %get-tuple-element.11.cols, f32[2,128,128]{2,1,0:T(8,128)S(1)} %get-tuple-element.12.inv, f32[2,128,128]{2,1,0:T(8,128)S(1)} %get-tuple-element.13.low, ...), custom_call_target="tpu_custom_call" | custom-call | tf_op jit(solution)/shard_map/apply_panels/pallas_call | solution.py:428
Async XLA Ops:
  0.0 1.2 %copy-start = (f32[2,8,128,128]{3,2,1,0:T(8,128)S(1)}, f32[2,8,128,128]{3,2,1,0:T(8,128)}, u32[]{:S(2)}) copy-start(f32[2,8,128,128]{3,2,1,0:T(8,128)} %mat.1) | copy-start | bytes 3145732
  1.2 0.7 %copy-start.1 = (s32[64]{0:T(128)S(1)}, s32[64]{0:T(128)}, u32[]{:S(2)}) copy-start(s32[64]{0:T(128)} %co.1) | copy-start | bytes 772
  1.9 0.7 %copy-start.2 = (s32[64]{0:T(128)S(1)}, s32[64]{0:T(128)}, u32[]{:S(2)}) copy-start(s32[64]{0:T(128)} %ro.1) | copy-start | bytes 772
  58.3 0.7 %copy-start.3 = (s32[2,64]{1,0:T(2,128)S(1)}, s32[2,64]{1,0:T(2,128)}, u32[]{:S(2)}) copy-start(s32[2,64]{1,0:T(2,128)} %pat.1) | copy-start | bytes 1540

commit v3 on v2

v3 whole, which is shorter than its diff:
```python
import functools

import jax
import jax.numpy as jnp
from jax import lax
from jax.experimental import pallas as pl
from jax.experimental.pallas import tpu as pltpu
from jax.sharding import PartitionSpec as P

MESH = pl.DeviceIdType.MESH
F32 = jnp.float32
PRECISE = lax.Precision.HIGHEST
W = 128
NODES = 64


def my_place():
    col = lax.axis_index("col")
    row = lax.axis_index("row")
    return col // 16, (col // 2) % 8, col % 2, row // 4, row % 4


def device(xh, z, k, xl, y):
    return {"col": (xh * 8 + z) * 2 + k, "row": xl * 4 + y}


def send_all(count, me, source, slot, target, send_sem, recv_sem):
    def step(q, carry):
        @pl.when(q != me)
        def _():
            pltpu.make_async_remote_copy(
                src_ref=source(q),
                dst_ref=slot(me),
                send_sem=send_sem.at[q],
                recv_sem=recv_sem.at[me],
                device_id=target(q),
                device_id_type=MESH,
            ).start()

        return carry

    lax.fori_loop(0, count, step, 0)


def recv_all(count, me, source, slot, target, send_sem, recv_sem):
    def step(q, carry):
        @pl.when(q != me)
        def _():
            copy = pltpu.make_async_remote_copy(
                src_ref=source(q),
                dst_ref=slot(q),
                send_sem=send_sem.at[q],
                recv_sem=recv_sem.at[q],
                device_id=target(q),
                device_id_type=MESH,
            )
            copy.wait_send()
            copy.wait_recv()

        return carry

    lax.fori_loop(0, count, step, 0)


def place_lead(diag, t, dst):
    for k in range(2):
        for q in range(16):
            dst[64 * k + 4 * q : 64 * k + 4 * q + 4, :] = diag[k, q, t]


FAR_FIRST = (4, 3, 5, 2, 6, 1, 7)


def comm_kernel(
    mat_hbm, co_hbm, ro_hbm, pat_hbm, base, fh, fl, inv, f01_out, cols, info,
    mat, co, ro, pat, st1, rc1, stl, rcl, half, leadh, rx, stz, rc2, pc2, za, xa, zb, xb, rows, cst, rc3, pc3, cbuf,
    dst1, rd1, pd1, rd2, diag, wa, wb, tile_a, low, f0,
    ld, s1, r1, sx, rxs, s2, r2, s4, r4, s4x, r4x, s5, r5, s6, r6, s7, r7,
    d1, e1, d2, e2, d3, e3, d4, e4,
):
    xh, z, k, xl, y = my_place()
    me_plane = (xh * 2 + xl) * 4 + y
    me_row = xl * 4 + y

    def plane(q):
        return device(q // 8, z, k, (q // 4) % 2, q % 4)

    def along(q):
        return device(xh, q, k, xl, y)

    def row_of(q):
        return device(xh, z, k, q // 4, q % 4)

    sib = device(xh, z, 1 - k, xl, y)
    partner = device(1 - xh, z, k, xl, y)

    def remote(src, dst, send, recv, target):
        return pltpu.make_async_remote_copy(
            src_ref=src, dst_ref=dst, send_sem=send, recv_sem=recv, device_id=target, device_id_type=MESH
        )

    barrier = pltpu.get_barrier_semaphore()

    def greet(count, me, target):
        def step(q, carry):
            @pl.when(q != me)
            def _():
                pl.semaphore_signal(barrier, inc=1, device_id=target(q), device_id_type=MESH)

            return carry

        lax.fori_loop(0, count, step, 0)

    greet(16, me_plane, plane)
    greet(8, z, along)
    pl.semaphore_signal(barrier, inc=1, device_id=sib, device_id_type=MESH)
    loads = [
        pltpu.make_async_copy(src, dst, ld.at[i])
        for i, (src, dst) in enumerate(((co_hbm, co), (ro_hbm, ro), (pat_hbm, pat), (mat_hbm, mat)))
    ]
    for copy in loads:
        copy.start()
    for copy in loads:
        copy.wait()

    owner = [co[p] // 2 for p in range(2)]
    local = [co[p] % 2 for p in range(2)]
    o_xh = [o // 16 for o in owner]
    o_z = [(o // 2) % 8 for o in owner]
    o_k = [o % 2 for o in owner]
    lead = ((0, 0), (0, 1), (1, 1))
    for p in range(2):
        st1[p] = mat[local[p], pl.ds(4 * (1 - k), 4)]
    for t, (p, n) in enumerate(lead):
        stl[t] = mat[local[p], ro[n] % 8, pl.ds(64 * (1 - k), 64), :]

    first_col = 2 * ((xh * 8 + z) * 2 + k)
    first_row = 8 * me_row

    def find(n, carry):
        c = co[n] - first_col
        s = ro[n]
        out = []
        for l in range(2):
            out.append(carry[l] + jnp.where(c == l, s, 0))
        for l in range(2):
            out.append(carry[2 + l] + jnp.where(c == l, n, 0))
        for i in range(8):
            out.append(carry[4 + i] + jnp.where(s - first_row == i, n, 0))
        return tuple(out)

    found = lax.fori_loop(0, NODES, find, (jnp.int32(0),) * 12)
    slots = [n % NODES for n in found[:2]]
    col_node = [n % NODES for n in found[2:4]]
    row_node = [n % NODES for n in found[4:]]
    keep_row = [[pat[p, n] == 1 for n in row_node] for p in range(2)]
    pl.semaphore_wait(barrier, 15 + 7 + 1)

    split_lead = remote(stl, rcl, s1.at[0], r1.at[0], sib)
    split_half = remote(st1, rc1, s1.at[1], r1.at[1], sib)
    split_lead.start()
    split_half.start()
    split_lead.wait()
    for t, (p, n) in enumerate(lead):
        mine = mat[local[p], ro[n] % 8, pl.ds(64 * k, 64), :]
        leadh[t] = jnp.where(o_k[p] == k, mine, rcl[t])
        for q in range(16):
            dst1[q, t] = leadh[t, 4 * q : 4 * q + 4, :]
    rd1[me_plane] = dst1[me_plane]
    d1_args = (16, me_plane, lambda q: dst1.at[q], lambda q: rd1.at[q], plane, d1, e1)
    send_all(*d1_args)
    split_half.wait()
    for p in range(2):
        mine = mat[local[p], pl.ds(4 * k, 4)]
        half[pl.ds(4 * p, 4)] = jnp.where(o_k[p] == k, mine, rc1[p])

    def cross(d):
        source = half.at[(z + d) % 8, pl.ds(64 * (1 - xh), 64), :]
        return remote(source, rx.at[d], sx.at[d], rxs.at[d], partner)

    def deal(d):
        return remote(stz.at[d], rc2.at[d], s2.at[d], r2.at[d], along((z + d) % 8))

    def scatter(d):
        zz = (z + d) % 8
        cross(d).wait_recv()
        own = jnp.where(zz < 4, o_xh[0], o_xh[1]) == xh
        value = jnp.where(own, half[zz, pl.ds(64 * xh, 64), :], rx[d])
        if d == 0:
            rc2[0] = value
        else:
            stz[d] = value
            deal(d).start()

    for d in FAR_FIRST + (0,):
        cross(d).start()
    for d in FAR_FIRST[:4]:
        scatter(d)
    recv_all(*d1_args)
    for t, (p, n) in enumerate(lead):
        slot = ro[n] // 8
        pd1[t] = rd1[(o_xh[p] * 2 + slot // 4) * 4 + slot % 4, t]
    rd2[z] = pd1[...]
    d2_args = (8, z, lambda q: pd1, lambda q: rd2.at[q], along, d2, e2)
    send_all(*d2_args)
    for d in FAR_FIRST[4:] + (0,):
        scatter(d)
    recv_all(*d2_args)
    for t, (p, n) in enumerate(lead):
        diag[k, me_plane, t] = rd2[o_z[p], t]
    d3_args = (16, me_plane, lambda q: diag.at[k, me_plane], lambda q: diag.at[k, q], plane, d3, e3)
    send_all(*d3_args)
    for d in FAR_FIRST:
        deal(d).wait()
    piece = rc2[(z + 8 - jnp.where(z < 4, o_z[0], o_z[1])) % 8]
    pc2[...] = piece

    def spread(d):
        return remote(pc2, za.at[d], s4.at[d], r4.at[d], along((z + d) % 8))

    def hand_over(d):
        return remote(za.at[d], xa.at[d], s4x.at[d], r4x.at[d], partner)

    za[0] = piece
    for d in FAR_FIRST:
        spread(d).start()
    hand_over(0).start()
    recv_all(*d3_args)
    remote(diag.at[k], diag.at[k], d4, e4, sib).start()

    for d in FAR_FIRST:
        spread(d).wait()
        hand_over(d).start()
    remote(za, zb, s5.at[0], r5.at[0], sib).start()
    joined_lead = remote(diag.at[k], diag.at[1 - k], d4, e4, sib)
    joined_lead.wait_send()
    joined_lead.wait_recv()

    rid = lax.broadcasted_iota(jnp.int32, (W, W), 0)
    cid = lax.broadcasted_iota(jnp.int32, (W, W), 1)
    eye = jnp.where(rid == cid, 1.0, 0.0).astype(F32)
    place_lead(diag, 0, wa)
    wb[...] = eye
    factor(wa, wb, 0, 6)

    for d in range(8):
        hand_over(d).wait()
        cross(d).wait_send()
    remote(xa, xb, s5.at[1], r5.at[1], sib).start()
    factor(wa, wb, 6, 16)
    low[0] = jnp.where(rid <= cid, wa[...], 0.0).T
    inv0 = wb[...]
    inv[0] = inv0
    remote(za, zb, s5.at[0], r5.at[0], sib).wait()
    remote(xa, xb, s5.at[1], r5.at[1], sib).wait()
    for d in range(8):
        t = (z + 8 - d) % 8
        for core, pieces in ((k, (za, xa)), (1 - k, (zb, xb))):
            rows[t // 4, 4 * core + t % 4, pl.ds(64 * xh, 64), :] = pieces[0][d]
            rows[t // 4, 4 * core + t % 4, pl.ds(64 * (1 - xh), 64), :] = pieces[1][d]

    for p in range(2):
        for l in range(2):
            tile = rows[p, slots[l] % 8]
            cst[4 * p + 2 * l] = tile[:64]
            cst[4 * p + 2 * l + 1] = tile[64:]
    rc3[me_row] = cst[me_row]
    c1_args = (8, me_row, lambda q: cst.at[q], lambda q: rc3.at[q], row_of, s6, r6)
    send_all(*c1_args)

    place_lead(diag, 1, tile_a)
    f01 = nt(tile_a[...], inv0)
    f01_out[...] = f01
    place_lead(diag, 2, wa)
    wa[...] = wa[...] - nt(f01, f01)
    wb[...] = eye
    factor(wa, wb, 0, 16)
    low[1] = jnp.where(rid <= cid, wa[...], 0.0).T
    inv[1] = wb[...]

    recv_all(*c1_args)
    piece = rc3[jnp.where((me_row // 2) % 2 == 0, slots[0] // 8, slots[1] // 8)]
    pc3[...] = piece
    cbuf[me_row] = piece
    c2_args = (8, me_row, lambda q: pc3, lambda q: cbuf.at[q], row_of, s7, r7)
    send_all(*c2_args)

    def mask(value, keeps):
        return jnp.concatenate(
            [jnp.where(keep, value[W * i : W * i + W], 0.0) for i, keep in enumerate(keeps)], axis=0
        )

    f0[...] = mask(nt3(rows[0].reshape(8 * W, W), inv[0]), keep_row[0])
    fh[:, :W], fl[:, :W] = parts(f0[...])
    f1 = mask(nt3(rows[1].reshape(8 * W, W) - nt3(f0[...], f01_out[...]), inv[1]), keep_row[1])
    fh[:, W:], fl[:, W:] = parts(f1)
    for l in range(2):
        first = col_node[l] == 0
        second = col_node[l] == 1
        for s in range(8):
            rows_s = slice(W * s, W * s + W)
            here = ((first & keep_row[0][s]), (second & keep_row[1][s]))
            edge = ((first & (row_node[s] == 0)), (second & (row_node[s] == 1)))
            tile = mat[l, s]
            tile = jnp.where(here[0], f0[rows_s], tile)
            tile = jnp.where(here[1], f1[rows_s], tile)
            tile = jnp.where(edge[0], low[0], tile)
            base[l, s] = jnp.where(edge[1], low[1], tile)
            fixed = here[0] | here[1] | edge[0] | edge[1]
            change = (row_node[s] >= col_node[l]) & jnp.logical_not(fixed)
            i = 8 * l + s
            info[i : i + 1, :] = jnp.where(change, jnp.ones((1, W), F32), 0.0)
    for p in range(2):
        for l in range(2):
            i = 16 + 2 * p + l
            info[i : i + 1, :] = jnp.where(pat[p, col_node[l]] == 1, jnp.ones((1, W), F32), 0.0)
    info[20:, :] = jnp.zeros((4, W), F32)
    recv_all(*c2_args)
    cols[...] = cbuf[...]


def gather_tiles(mat, co, ro, pat):
    vmem = pl.BlockSpec(memory_space=pltpu.VMEM)
    hbm = pl.BlockSpec(memory_space=pltpu.HBM)
    dma = pltpu.SemaphoreType.DMA
    vm = lambda *shape: pltpu.VMEM(shape, F32)
    pair = lambda n: [dma((n,)), dma((n,))]
    out = lambda *shape, dtype=F32: jax.ShapeDtypeStruct(shape, dtype)
    return pl.pallas_call(
        comm_kernel,
        out_shape=(
            out(2, 8, W, W),
            out(8 * W, 2 * W, dtype=jnp.bfloat16),
            out(8 * W, 2 * W, dtype=jnp.bfloat16),
            out(2, W, W),
            out(W, W),
            out(8, 64, W),
            out(24, W),
        ),
        in_specs=[hbm] * 4,
        out_specs=(vmem,) * 7,
        scratch_shapes=[
            vm(2, 8, W, W),
            pltpu.SMEM((NODES,), jnp.int32),
            pltpu.SMEM((NODES,), jnp.int32),
            pltpu.SMEM((2, NODES), jnp.int32),
            vm(2, 4, W, W), vm(2, 4, W, W),
            vm(3, 64, W), vm(3, 64, W),
            vm(8, W, W), vm(3, 64, W),
            vm(8, 64, W), vm(8, 64, W), vm(8, 64, W), vm(64, W),
            vm(8, 64, W), vm(8, 64, W), vm(8, 64, W), vm(8, 64, W), vm(2, 8, W, W),
            vm(8, 64, W), vm(8, 64, W), vm(64, W), vm(8, 64, W),
            vm(16, 3, 4, W), vm(16, 3, 4, W), vm(3, 4, W), vm(8, 3, 4, W), vm(2, 16, 3, 4, W),
            vm(W, W), vm(W, W), vm(W, W), vm(2, W, W), vm(8 * W, W),
            dma((4,)),
            *pair(2), *pair(8), *pair(8), *pair(8), *pair(8), *pair(2), *pair(8), *pair(8),
            *pair(16), *pair(8), *pair(16), dma, dma,
        ],
        compiler_params=pltpu.CompilerParams(
            collective_id=0, has_side_effects=True, vmem_limit_bytes=40 * 1024 * 1024
        ),
        name="gather_tiles",
    )(mat, co, ro, pat)


def lanes(x):
    return jnp.broadcast_to(x, (x.shape[0], W))


def subs(x):
    return jnp.broadcast_to(x, (8, W))


def factor(wa_ref, wb_ref, first, last):
    rid = lax.broadcasted_iota(jnp.int32, (8, W), 0)
    for c in range(8 * first, 8 * last, 8):
        wa = wa_ref[c : c + 8, :]
        wb = wb_ref[c : c + 8, :]
        cl = [lanes(wa[:, c + i : c + i + 1]) for i in range(8)]
        pa, pb, sc, lt = [], [], [], []
        for i in range(8):
            s = lax.rsqrt(subs(cl[i][i : i + 1]))
            li = cl[i] * s
            ra = subs(wa[i : i + 1]) * s
            rb = subs(wb[i : i + 1]) * s
            low = jnp.where(rid > i, li, 0.0)
            wa = jnp.where(rid == i, ra, wa - low * ra)
            wb = jnp.where(rid == i, rb, wb - low * rb)
            row = {}
            for j in range(i + 1, 8):
                row[j] = subs(li[j : j + 1])
                cl[j] = cl[j] - li * row[j]
            pa.append(ra)
            pb.append(rb)
            sc.append(s)
            lt.append(row)
        wa_ref[c : c + 8, :] = wa
        wb_ref[c : c + 8, :] = wb
        g = c + 8
        while g < W:
            size = min(16, W - g)
            tile = lambda v: jnp.concatenate([v] * (size // 8), axis=0) if size > 8 else v
            ga = wa_ref[g : g + size, :]
            gb = wb_ref[g : g + size, :]
            gc = [lanes(ga[:, c + i : c + i + 1]) for i in range(8)]
            for i in range(8):
                li = gc[i] * tile(sc[i])
                ga = ga - li * tile(pa[i])
                gb = gb - li * tile(pb[i])
                for j in range(i + 1, 8):
                    gc[j] = gc[j] - li * tile(lt[i][j])
            wa_ref[g : g + size, :] = ga
            wb_ref[g : g + size, :] = gb
            g += size


def nt(a, b):
    return lax.dot_general(a, b, (((1,), (1,)), ((), ())), precision=PRECISE, preferred_element_type=F32)


def nt16(a, b):
    return lax.dot_general(a, b, (((1,), (1,)), ((), ())), preferred_element_type=F32)


def parts(a):
    high = a.astype(jnp.bfloat16)
    return high, (a - high.astype(F32)).astype(jnp.bfloat16)


def nt3(a, b):
    ah, al = parts(a)
    bh, bl = parts(b)
    both = nt16(jnp.concatenate([ah, al], axis=1), jnp.concatenate([bh, bh], axis=1))
    return both + nt16(ah, bl)


def apply_kernel(base, fh, fl, inv, f01, cols, info, out, buf, sem):
    def flag(i):
        return info[i : i + 1, :] > 0.5

    def mask(value, p):
        return jnp.concatenate(
            [jnp.where(flag(16 + 2 * p + l), value[W * l : W * l + W], 0.0) for l in range(2)], axis=0
        )

    raw = lambda p: cols[4 * p : 4 * p + 4].reshape(2 * W, W)
    g0 = mask(nt3(raw(0), inv[0]), 0)
    g1 = mask(nt3(raw(1) - nt3(g0, f01[...]), inv[1]), 1)
    g0h, g0l = parts(g0)
    g1h, g1l = parts(g1)
    gh = jnp.concatenate([g0h, g1h], axis=1)
    gl = jnp.concatenate([g0l, g1l], axis=1)
    copies = []
    for s in range(0, 8, 2):
        both = slice(W * s, W * s + 2 * W)
        step = nt16(fh[both], gh) + nt16(fl[both], gh) + nt16(fh[both], gl)
        for l in range(2):
            for i in range(2):
                old = base[l, s + i]
                new = old - step[W * i : W * i + W, W * l : W * l + W]
                buf[l, s + i] = jnp.where(flag(8 * l + s + i), new, old)
            copy = pltpu.make_async_copy(buf.at[l, pl.ds(s, 2)], out.at[l, pl.ds(s, 2)], sem.at[l + s])
            copy.start()
            copies.append(copy)
    for copy in copies:
        copy.wait()


def apply_panels(base, fh, fl, inv, f01, cols, info):
    vmem = pl.BlockSpec(memory_space=pltpu.VMEM)
    return pl.pallas_call(
        apply_kernel,
        out_shape=jax.ShapeDtypeStruct((2, 8, W, W), F32),
        in_specs=[vmem] * 7,
        out_specs=pl.BlockSpec(memory_space=pltpu.HBM),
        scratch_shapes=[pltpu.VMEM((2, 8, W, W), F32), pltpu.SemaphoreType.DMA((8,))],
        compiler_params=pltpu.CompilerParams(vmem_limit_bytes=16 * 1024 * 1024),
        name="apply_panels",
    )(base, fh, fl, inv, f01, cols, info)


def body(matrix, col_owner, row_owner, pattern):
    held = [pltpu.with_memory_space_constraint(x, pltpu.HBM) for x in (matrix, col_owner, row_owner, pattern)]
    return apply_panels(*gather_tiles(*held))


def solution(mesh):
    return jax.shard_map(
        body,
        mesh=mesh,
        in_specs=(P("col", "row", None, None), P(), P(), P()),
        out_specs=P("col", "row", None, None),
        check_vma=False,
    )
```

time: 64 us -> 53.5 us (0.84)
  Pallas kernels: 60.2 us -> 52.5 us
  local copies, waits for them, and re-layouts: 3.21 us -> 0 us
    pallas_call x1, Pallas kernels: 55.8 us -> 50.5 us  [gather_tiles(): pl.pallas_call(comm_kernel, out_shape=(out(2, 8, W, W), out(8 * W, 2 * W,...]
    unnamed x8 -> x0, local copies, waits for them, and re-layouts: 3.21 us -> none
    pallas_call x1, Pallas kernels: 4.4 us -> 2.03 us  [apply_panels(): pl.pallas_call(apply_kernel, out_shape=jax.ShapeDtypeStruct((2, 8, W, W),...]
where the time goes in v3:
time: 53.5 us; the launch traced here: 52.5 us
  Pallas kernels  52.5 us (98%)
    pallas_call x1, Pallas kernels, gather_tiles(): pl.pallas_call(comm_kernel, out_shape=(out(2, 8, W, W), out(8 * W, 2 * W,...  50.5 us
    pallas_call x1, Pallas kernels, apply_panels(): pl.pallas_call(apply_kernel, out_shape=jax.ShapeDtypeStruct((2, 8, W, W),...  2.03 us

profile of v3, /device:TPU:1, one launch (start us, length us, event | category | flops | bytes accessed | tf_op | source)
XLA Modules:
  0.0 52.5 jit_solution(16132948677368390737)
XLA Ops:
  0.0 50.5 %gather_tiles.1 = (f32[2,8,128,128]{3,2,1,0:T(8,128)S(1)}, bf16[1024,256]{1,0:T(8,128)(2,1)S(1)}, bf16[1024,256]{1,0:T(8,128)(2,1)S(1)}, f32[2,128,128]{2,1,0:T(...) custom-call(f32[2,8,128,128]{3,2,1,0:T(8,128)} %mat_hbm.1, s32[64]{0:T(128)} %co_hbm.1, ...), custom_call_target="tpu_custom_call" | custom-call | tf_op jit(solution)/shard_map/gather_tiles/pallas_call | solution.py:329
  50.5 2.0 %apply_panels.1 = f32[2,8,128,128]{3,2,1,0:T(8,128)} custom-call(f32[2,8,128,128]{3,2,1,0:T(8,128)S(1)} %get-tuple-element.12.base, bf16[1024,256]{1,0:T(8,128)(2,1)S(1)} %get-tuple-element.13.fh, bf16[1024,256]{1,0:T(8,128)(2,1)S(1)} %get-tuple-element.14.fl, f32[2,128,128]{2,1,0:T(8,128)S(1)} %get-tuple-element.15.inv, ...), custom_call_target="tpu_custom_call" | custom-call | tf_op jit(solution)/shard_map/apply_panels/pallas_call | solution.py:471

commit v4 on v3

--- a/solution.py
+++ b/solution.py
@@ -42,7 +42,7 @@
     lax.fori_loop(0, count, step, 0)
 
 
-def recv_all(count, me, source, slot, target, send_sem, recv_sem):
+def wait_all(count, me, source, slot, target, send_sem, recv_sem, sent=False):
     def step(q, carry):
         @pl.when(q != me)
         def _():
@@ -54,12 +54,22 @@
                 device_id=target(q),
                 device_id_type=MESH,
             )
-            copy.wait_send()
-            copy.wait_recv()
+            if sent:
+                copy.wait_send()
+            else:
+                copy.wait_recv()
 
         return carry
 
     lax.fori_loop(0, count, step, 0)
+
+
+def recv_all(*args):
+    wait_all(*args)
+
+
+def sent_all(*args):
+    wait_all(*args, sent=True)
 
 
 def place_lead(diag, t, dst):
@@ -73,11 +83,17 @@
 
 def comm_kernel(
     mat_hbm, co_hbm, ro_hbm, pat_hbm, base, fh, fl, inv, f01_out, cols, info,
-    mat, co, ro, pat, st1, rc1, stl, rcl, half, leadh, rx, stz, rc2, pc2, za, xa, zb, xb, rows, cst, rc3, pc3, cbuf,
+    mat, co, ro, pat, st1, rc1, stl, rcl, half, leadh, rows,
+    rx0, rx1, stz0, stz1, rc20, rc21, pc20, pc21, za0, za1, xa0, xa1, zb0, zb1, xb0, xb1,
+    cst0, cst1, rc30, rc31, pc30, pc31, cbuf0, cbuf1,
     dst1, rd1, pd1, rd2, diag, wa, wb, tile_a, low, f0,
     ld, s1, r1, sx, rxs, s2, r2, s4, r4, s4x, r4x, s5, r5, s6, r6, s7, r7,
     d1, e1, d2, e2, d3, e3, d4, e4,
 ):
+    rx, stz, rc2, pc2 = (rx0, rx1), (stz0, stz1), (rc20, rc21), (pc20, pc21)
+    za, xa, zb, xb = (za0, za1), (xa0, xa1), (zb0, zb1), (xb0, xb1)
+    cst, rc3, pc3, cbuf = (cst0, cst1), (rc30, rc31), (pc30, pc31), (cbuf0, cbuf1)
+    waves = (0, 1)
     xh, z, k, xl, y = my_place()
     me_plane = (xh * 2 + xl) * 4 + y
     me_row = xl * 4 + y
@@ -99,27 +115,28 @@
             src_ref=src, dst_ref=dst, send_sem=send, recv_sem=recv, device_id=target, device_id_type=MESH
         )
 
-    barrier = pltpu.get_barrier_semaphore()
-
-    def greet(count, me, target):
-        def step(q, carry):
-            @pl.when(q != me)
-            def _():
-                pl.semaphore_signal(barrier, inc=1, device_id=target(q), device_id_type=MESH)
-
-            return carry
-
-        lax.fori_loop(0, count, step, 0)
-
-    greet(16, me_plane, plane)
-    greet(8, z, along)
-    pl.semaphore_signal(barrier, inc=1, device_id=sib, device_id_type=MESH)
     loads = [
         pltpu.make_async_copy(src, dst, ld.at[i])
         for i, (src, dst) in enumerate(((co_hbm, co), (ro_hbm, ro), (pat_hbm, pat), (mat_hbm, mat)))
     ]
     for copy in loads:
         copy.start()
+
+    barrier = pltpu.get_barrier_semaphore()
+
+    def greet(count, me, target):
+        def step(q, carry):
+            @pl.when(q != me)
+            def _():
+                pl.semaphore_signal(barrier, inc=1, device_id=target(q), device_id_type=MESH)
+
+            return carry
+
+        lax.fori_loop(0, count, step, 0)
+
+    greet(16, me_plane, plane)
+    greet(8, z, along)
+    pl.semaphore_signal(barrier, inc=1, device_id=sib, device_id_type=MESH)
     for copy in loads:
         copy.wait()
 
@@ -133,6 +150,48 @@
         st1[p] = mat[local[p], pl.ds(4 * (1 - k), 4)]
     for t, (p, n) in enumerate(lead):
         stl[t] = mat[local[p], ro[n] % 8, pl.ds(64 * (1 - k), 64), :]
+
+    pl.semaphore_wait(barrier, 15 + 7 + 1)
+
+    split_lead = remote(stl, rcl, s1.at[0], r1.at[0], sib)
+    split_half = remote(st1, rc1, s1.at[1], r1.at[1], sib)
+    split_lead.start()
+    split_half.start()
+    split_lead.wait_recv()
+    for t, (p, n) in enumerate(lead):
+        mine = mat[local[p], ro[n] % 8, pl.ds(64 * k, 64), :]
+        leadh[t] = jnp.where(o_k[p] == k, mine, rcl[t])
+        for q in range(16):
+            dst1[q, t] = leadh[t, 4 * q : 4 * q + 4, :]
+    rd1[me_plane] = dst1[me_plane]
+    d1_args = (16, me_plane, lambda q: dst1.at[q], lambda q: rd1.at[q], plane, d1, e1)
+    send_all(*d1_args)
+    split_half.wait_recv()
+    for p in range(2):
+        mine = mat[local[p], pl.ds(4 * k, 4)]
+        half[pl.ds(4 * p, 4)] = jnp.where(o_k[p] == k, mine, rc1[p])
+
+    def cross(d, w):
+        source = half.at[(z + d) % 8, pl.ds(64 * (1 - xh) + 32 * w, 32), :]
+        return remote(source, rx[w].at[d], sx.at[w, d], rxs.at[w, d], partner)
+
+    def deal(d, w):
+        return remote(stz[w].at[d], rc2[w].at[d], s2.at[w, d], r2.at[w, d], along((z + d) % 8))
+
+    def scatter(d, w):
+        zz = (z + d) % 8
+        cross(d, w).wait_recv()
+        own = jnp.where(zz < 4, o_xh[0], o_xh[1]) == xh
+        value = jnp.where(own, half[zz, pl.ds(64 * xh + 32 * w, 32), :], rx[w][d])
+        if d == 0:
+            rc2[w][0] = value
+        else:
+            stz[w][d] = value
+            deal(d, w).start()
+
+    for w in waves:
+        for d in FAR_FIRST + (0,):
+            cross(d, w).start()
 
     first_col = 2 * ((xh * 8 + z) * 2 + k)
     first_row = 8 * me_row
@@ -154,48 +213,9 @@
     col_node = [n % NODES for n in found[2:4]]
     row_node = [n % NODES for n in found[4:]]
     keep_row = [[pat[p, n] == 1 for n in row_node] for p in range(2)]
-    pl.semaphore_wait(barrier, 15 + 7 + 1)
-
-    split_lead = remote(stl, rcl, s1.at[0], r1.at[0], sib)
-    split_half = remote(st1, rc1, s1.at[1], r1.at[1], sib)
-    split_lead.start()
-    split_half.start()
-    split_lead.wait()
-    for t, (p, n) in enumerate(lead):
-        mine = mat[local[p], ro[n] % 8, pl.ds(64 * k, 64), :]
-        leadh[t] = jnp.where(o_k[p] == k, mine, rcl[t])
-        for q in range(16):
-            dst1[q, t] = leadh[t, 4 * q : 4 * q + 4, :]
-    rd1[me_plane] = dst1[me_plane]
-    d1_args = (16, me_plane, lambda q: dst1.at[q], lambda q: rd1.at[q], plane, d1, e1)
-    send_all(*d1_args)
-    split_half.wait()
-    for p in range(2):
-        mine = mat[local[p], pl.ds(4 * k, 4)]
-        half[pl.ds(4 * p, 4)] = jnp.where(o_k[p] == k, mine, rc1[p])
-
-    def cross(d):
-        source = half.at[(z + d) % 8, pl.ds(64 * (1 - xh), 64), :]
-        return remote(source, rx.at[d], sx.at[d], rxs.at[d], partner)
-
-    def deal(d):
-        return remote(stz.at[d], rc2.at[d], s2.at[d], r2.at[d], along((z + d) % 8))
-
-    def scatter(d):
-        zz = (z + d) % 8
-        cross(d).wait_recv()
-        own = jnp.where(zz < 4, o_xh[0], o_xh[1]) == xh
-        value = jnp.where(own, half[zz, pl.ds(64 * xh, 64), :], rx[d])
-        if d == 0:
-            rc2[0] = value
-        else:
-            stz[d] = value
-            deal(d).start()
 
     for d in FAR_FIRST + (0,):
-        cross(d).start()
-    for d in FAR_FIRST[:4]:
-        scatter(d)
+        scatter(d, 0)
     recv_all(*d1_args)
     for t, (p, n) in enumerate(lead):
         slot = ro[n] // 8
@@ -203,37 +223,44 @@
     rd2[z] = pd1[...]
     d2_args = (8, z, lambda q: pd1, lambda q: rd2.at[q], along, d2, e2)
     send_all(*d2_args)
-    for d in FAR_FIRST[4:] + (0,):
-        scatter(d)
+    for d in FAR_FIRST + (0,):
+        scatter(d, 1)
+
+    def spread(d, w):
+        return remote(pc2[w], za[w].at[d], s4.at[w, d], r4.at[w, d], along((z + d) % 8))
+
+    def hand_over(d, w):
+        return remote(za[w].at[d], xa[w].at[d], s4x.at[w, d], r4x.at[w, d], partner)
+
+    def start_gather(w):
+        for d in FAR_FIRST:
+            deal(d, w).wait_recv()
+        piece = rc2[w][(z + 8 - jnp.where(z < 4, o_z[0], o_z[1])) % 8]
+        pc2[w][...] = piece
+        za[w][0] = piece
+        for d in FAR_FIRST:
+            spread(d, w).start()
+        hand_over(0, w).start()
+
+    start_gather(0)
     recv_all(*d2_args)
     for t, (p, n) in enumerate(lead):
         diag[k, me_plane, t] = rd2[o_z[p], t]
     d3_args = (16, me_plane, lambda q: diag.at[k, me_plane], lambda q: diag.at[k, q], plane, d3, e3)
     send_all(*d3_args)
-    for d in FAR_FIRST:
-        deal(d).wait()
-    piece = rc2[(z + 8 - jnp.where(z < 4, o_z[0], o_z[1])) % 8]
-    pc2[...] = piece
-
-    def spread(d):
-        return remote(pc2, za.at[d], s4.at[d], r4.at[d], along((z + d) % 8))
-
-    def hand_over(d):
-        return remote(za.at[d], xa.at[d], s4x.at[d], r4x.at[d], partner)
-
-    za[0] = piece
-    for d in FAR_FIRST:
-        spread(d).start()
-    hand_over(0).start()
+    start_gather(1)
     recv_all(*d3_args)
     remote(diag.at[k], diag.at[k], d4, e4, sib).start()
 
-    for d in FAR_FIRST:
-        spread(d).wait()
-        hand_over(d).start()
-    remote(za, zb, s5.at[0], r5.at[0], sib).start()
+    def join(src, dst, i, w):
+        return remote(src[w], dst[w], s5.at[i, w], r5.at[i, w], sib)
+
+    for w in waves:
+        for d in FAR_FIRST:
+            spread(d, w).wait_recv()
+            hand_over(d, w).start()
+        join(za, zb, 0, w).start()
     joined_lead = remote(diag.at[k], diag.at[1 - k], d4, e4, sib)
-    joined_lead.wait_send()
     joined_lead.wait_recv()
 
     rid = lax.broadcasted_iota(jnp.int32, (W, W), 0)
@@ -241,33 +268,48 @@
     eye = jnp.where(rid == cid, 1.0, 0.0).astype(F32)
     place_lead(diag, 0, wa)
     wb[...] = eye
-    factor(wa, wb, 0, 6)
-
-    for d in range(8):
-        hand_over(d).wait()
-        cross(d).wait_send()
-    remote(xa, xb, s5.at[1], r5.at[1], sib).start()
-    factor(wa, wb, 6, 16)
+    factor(wa, wb, 0, 4)
+
+    def crossed(w):
+        for d in range(8):
+            hand_over(d, w).wait_recv()
+        join(xa, xb, 1, w).start()
+
+    def c1_args(w):
+        return 8, me_row, lambda q: cst[w].at[q], lambda q: rc3[w].at[q], row_of, s6.at[w], r6.at[w]
+
+    def c2_args(w):
+        return 8, me_row, lambda q: pc3[w], lambda q: cbuf[w].at[q], row_of, s7.at[w], r7.at[w]
+
+    def start_columns(w):
+        join(za, zb, 0, w).wait_recv()
+        join(xa, xb, 1, w).wait_recv()
+        for p in range(2):
+            for l in range(2):
+                i = slots[l] % 8
+                d = (z + 8 - 4 * p - i % 4) % 8
+                mine = i // 4 == k
+                cst[w][4 * p + 2 * l + xh] = jnp.where(mine, za[w][d], zb[w][d])
+                cst[w][4 * p + 2 * l + 1 - xh] = jnp.where(mine, xa[w][d], xb[w][d])
+        rc3[w][me_row] = cst[w][me_row]
+        send_all(*c1_args(w))
+
+    def pass_columns(w):
+        recv_all(*c1_args(w))
+        piece = rc3[w][jnp.where((me_row // 2) % 2 == 0, slots[0] // 8, slots[1] // 8)]
+        pc3[w][...] = piece
+        cbuf[w][me_row] = piece
+        send_all(*c2_args(w))
+
+    crossed(0)
+    factor(wa, wb, 4, 8)
+    crossed(1)
+    start_columns(0)
+    start_columns(1)
+    factor(wa, wb, 8, 16)
     low[0] = jnp.where(rid <= cid, wa[...], 0.0).T
     inv0 = wb[...]
     inv[0] = inv0
-    remote(za, zb, s5.at[0], r5.at[0], sib).wait()
-    remote(xa, xb, s5.at[1], r5.at[1], sib).wait()
-    for d in range(8):
-        t = (z + 8 - d) % 8
-        for core, pieces in ((k, (za, xa)), (1 - k, (zb, xb))):
-            rows[t // 4, 4 * core + t % 4, pl.ds(64 * xh, 64), :] = pieces[0][d]
-            rows[t // 4, 4 * core + t % 4, pl.ds(64 * (1 - xh), 64), :] = pieces[1][d]
-
-    for p in range(2):
-        for l in range(2):
-            tile = rows[p, slots[l] % 8]
-            cst[4 * p + 2 * l] = tile[:64]
-            cst[4 * p + 2 * l + 1] = tile[64:]
-    rc3[me_row] = cst[me_row]
-    c1_args = (8, me_row, lambda q: cst.at[q], lambda q: rc3.at[q], row_of, s6, r6)
-    send_all(*c1_args)
-
     place_lead(diag, 1, tile_a)
     f01 = nt(tile_a[...], inv0)
     f01_out[...] = f01
@@ -278,12 +320,14 @@
     low[1] = jnp.where(rid <= cid, wa[...], 0.0).T
     inv[1] = wb[...]
 
-    recv_all(*c1_args)
-    piece = rc3[jnp.where((me_row // 2) % 2 == 0, slots[0] // 8, slots[1] // 8)]
-    pc3[...] = piece
-    cbuf[me_row] = piece
-    c2_args = (8, me_row, lambda q: pc3, lambda q: cbuf.at[q], row_of, s7, r7)
-    send_all(*c2_args)
+    pass_columns(0)
+    pass_columns(1)
+    for d in range(8):
+        t = (z + 8 - d) % 8
+        for w in waves:
+            for core, pieces in ((k, (za, xa)), (1 - k, (zb, xb))):
+                rows[t // 4, 4 * core + t % 4, pl.ds(64 * xh + 32 * w, 32), :] = pieces[0][w][d]
+                rows[t // 4, 4 * core + t % 4, pl.ds(64 * (1 - xh) + 32 * w, 32), :] = pieces[1][w][d]
 
     def mask(value, keeps):
         return jnp.concatenate(
@@ -315,8 +359,23 @@
             i = 16 + 2 * p + l
             info[i : i + 1, :] = jnp.where(pat[p, col_node[l]] == 1, jnp.ones((1, W), F32), 0.0)
     info[20:, :] = jnp.zeros((4, W), F32)
-    recv_all(*c2_args)
-    cols[...] = cbuf[...]
+    for arguments in (d1_args, d2_args, d3_args, c1_args(0), c1_args(1), c2_args(0), c2_args(1)):
+        sent_all(*arguments)
+    for w in waves:
+        for d in range(8):
+            cross(d, w).wait_send()
+            hand_over(d, w).wait_send()
+            if d:
+                deal(d, w).wait_send()
+                spread(d, w).wait_send()
+        join(za, zb, 0, w).wait_send()
+        join(xa, xb, 1, w).wait_send()
+    for copy in (split_lead, split_half, joined_lead):
+        copy.wait_send()
+    for w in waves:
+        recv_all(*c2_args(w))
+        for q in range(8):
+            cols[q, 32 * w : 32 * w + 32, :] = cbuf[w][q]
 
 
 def gather_tiles(mat, co, ro, pat):
@@ -325,6 +384,7 @@
     dma = pltpu.SemaphoreType.DMA
     vm = lambda *shape: pltpu.VMEM(shape, F32)
     pair = lambda n: [dma((n,)), dma((n,))]
+    pairs = lambda n: [dma((2, n)), dma((2, n))]
     out = lambda *shape, dtype=F32: jax.ShapeDtypeStruct(shape, dtype)
     return pl.pallas_call(
         comm_kernel,
@@ -346,14 +406,13 @@
             pltpu.SMEM((2, NODES), jnp.int32),
             vm(2, 4, W, W), vm(2, 4, W, W),
             vm(3, 64, W), vm(3, 64, W),
-            vm(8, W, W), vm(3, 64, W),
-            vm(8, 64, W), vm(8, 64, W), vm(8, 64, W), vm(64, W),
-            vm(8, 64, W), vm(8, 64, W), vm(8, 64, W), vm(8, 64, W), vm(2, 8, W, W),
-            vm(8, 64, W), vm(8, 64, W), vm(64, W), vm(8, 64, W),
+            vm(8, W, W), vm(3, 64, W), vm(2, 8, W, W),
+            *[vm(8, 32, W)] * 6, *[vm(32, W)] * 2, *[vm(8, 32, W)] * 8,
+            *[vm(8, 32, W)] * 4, *[vm(32, W)] * 2, *[vm(8, 32, W)] * 2,
             vm(16, 3, 4, W), vm(16, 3, 4, W), vm(3, 4, W), vm(8, 3, 4, W), vm(2, 16, 3, 4, W),
             vm(W, W), vm(W, W), vm(W, W), vm(2, W, W), vm(8 * W, W),
             dma((4,)),
-            *pair(2), *pair(8), *pair(8), *pair(8), *pair(8), *pair(2), *pair(8), *pair(8),
+            *pair(2), *pairs(8), *pairs(8), *pairs(8), *pairs(8), *pairs(2), *pairs(8), *pairs(8),
             *pair(16), *pair(8), *pair(16), dma, dma,
         ],
         compiler_params=pltpu.CompilerParams(

time: 53.5 us -> 52.7 us (0.985); the launches traced: 52.5 us -> 52.6 us
  no operation moved by 1% of the time
where the time goes in v4:
time: 52.7 us; the launch traced here: 52.6 us
  Pallas kernels  52.6 us (100%)
    pallas_call x1, Pallas kernels, gather_tiles(): pl.pallas_call(comm_kernel, out_shape=(out(2, 8, W, W), out(8 * W, 2 * W,...  50.5 us
    pallas_call x1, Pallas kernels, apply_panels(): pl.pallas_call(apply_kernel, out_shape=jax.ShapeDtypeStruct((2, 8, W, W),...  2.04 us

profile of v4, /device:TPU:1, one launch (start us, length us, event | category | flops | bytes accessed | tf_op | source)
XLA Modules:
  0.0 52.6 jit_solution(4081948436629080480)
XLA Ops:
  0.0 50.5 %gather_tiles.1 = (f32[2,8,128,128]{3,2,1,0:T(8,128)S(1)}, bf16[1024,256]{1,0:T(8,128)(2,1)S(1)}, bf16[1024,256]{1,0:T(8,128)(2,1)S(1)}, f32[2,128,128]{2,1,0:T(...) custom-call(f32[2,8,128,128]{3,2,1,0:T(8,128)} %mat_hbm.1, s32[64]{0:T(128)} %co_hbm.1, ...), custom_call_target="tpu_custom_call" | custom-call | tf_op jit(solution)/shard_map/gather_tiles/pallas_call | solution.py:389
  50.6 2.0 %apply_panels.1 = f32[2,8,128,128]{3,2,1,0:T(8,128)} custom-call(f32[2,8,128,128]{3,2,1,0:T(8,128)S(1)} %get-tuple-element.12.base, bf16[1024,256]{1,0:T(8,128)(2,1)S(1)} %get-tuple-element.13.fh, bf16[1024,256]{1,0:T(8,128)(2,1)S(1)} %get-tuple-element.14.fl, f32[2,128,128]{2,1,0:T(8,128)S(1)} %get-tuple-element.15.inv, ...), custom_call_target="tpu_custom_call" | custom-call | tf_op jit(solution)/shard_map/apply_panels/pallas_call | solution.py:530

commit v5 on v4

--- a/solution.py
+++ b/solution.py
@@ -249,17 +249,20 @@
     d3_args = (16, me_plane, lambda q: diag.at[k, me_plane], lambda q: diag.at[k, q], plane, d3, e3)
     send_all(*d3_args)
     start_gather(1)
+
+    def join(src, dst, i, w):
+        return remote(src[w], dst[w], s5.at[i, w], r5.at[i, w], sib)
+
+    for d in FAR_FIRST:
+        spread(d, 0).wait_recv()
+        hand_over(d, 0).start()
+    join(za, zb, 0, 0).start()
     recv_all(*d3_args)
     remote(diag.at[k], diag.at[k], d4, e4, sib).start()
-
-    def join(src, dst, i, w):
-        return remote(src[w], dst[w], s5.at[i, w], r5.at[i, w], sib)
-
-    for w in waves:
-        for d in FAR_FIRST:
-            spread(d, w).wait_recv()
-            hand_over(d, w).start()
-        join(za, zb, 0, w).start()
+    for d in FAR_FIRST:
+        spread(d, 1).wait_recv()
+        hand_over(d, 1).start()
+    join(za, zb, 0, 1).start()
     joined_lead = remote(diag.at[k], diag.at[1 - k], d4, e4, sib)
     joined_lead.wait_recv()
 
@@ -268,7 +271,7 @@
     eye = jnp.where(rid == cid, 1.0, 0.0).astype(F32)
     place_lead(diag, 0, wa)
     wb[...] = eye
-    factor(wa, wb, 0, 4)
+    factor(wa, wb, 0, 6)
 
     def crossed(w):
         for d in range(8):
@@ -302,11 +305,12 @@
         send_all(*c2_args(w))
 
     crossed(0)
-    factor(wa, wb, 4, 8)
+    factor(wa, wb, 6, 9)
     crossed(1)
     start_columns(0)
+    factor(wa, wb, 9, 12)
     start_columns(1)
-    factor(wa, wb, 8, 16)
+    factor(wa, wb, 12, 16)
     low[0] = jnp.where(rid <= cid, wa[...], 0.0).T
     inv0 = wb[...]
     inv[0] = inv0
@@ -316,12 +320,13 @@
     place_lead(diag, 2, wa)
     wa[...] = wa[...] - nt(f01, f01)
     wb[...] = eye
-    factor(wa, wb, 0, 16)
+    factor(wa, wb, 0, 7)
+    pass_columns(0)
+    pass_columns(1)
+    factor(wa, wb, 7, 16)
     low[1] = jnp.where(rid <= cid, wa[...], 0.0).T
     inv[1] = wb[...]
 
-    pass_columns(0)
-    pass_columns(1)
     for d in range(8):
         t = (z + 8 - d) % 8
         for w in waves:

time: 52.7 us -> 50.3 us (0.954)
  Pallas kernels: 52.6 us -> 50.2 us
    pallas_call x1, Pallas kernels: 50.5 us -> 48.2 us  [gather_tiles(): pl.pallas_call(comm_kernel, out_shape=(out(2, 8, W, W), out(8 * W, 2 * W,...]
where the time goes in v5:
time: 50.3 us; the launch traced here: 50.2 us
  Pallas kernels  50.2 us (100%)
    pallas_call x1, Pallas kernels, gather_tiles(): pl.pallas_call(comm_kernel, out_shape=(out(2, 8, W, W), out(8 * W, 2 * W,...  48.2 us
    pallas_call x1, Pallas kernels, apply_panels(): pl.pallas_call(apply_kernel, out_shape=jax.ShapeDtypeStruct((2, 8, W, W),...  2.04 us

profile of v5, /device:TPU:1, one launch (start us, length us, event | category | flops | bytes accessed | tf_op | source)
XLA Modules:
  0.0 50.2 jit_solution(14924420446120340707)
XLA Ops:
  0.0 48.2 %gather_tiles.1 = (f32[2,8,128,128]{3,2,1,0:T(8,128)S(1)}, bf16[1024,256]{1,0:T(8,128)(2,1)S(1)}, bf16[1024,256]{1,0:T(8,128)(2,1)S(1)}, f32[2,128,128]{2,1,0:T(...) custom-call(f32[2,8,128,128]{3,2,1,0:T(8,128)} %mat_hbm.1, s32[64]{0:T(128)} %co_hbm.1, ...), custom_call_target="tpu_custom_call" | custom-call | tf_op jit(solution)/shard_map/gather_tiles/pallas_call | solution.py:394
  48.2 2.0 %apply_panels.1 = f32[2,8,128,128]{3,2,1,0:T(8,128)} custom-call(f32[2,8,128,128]{3,2,1,0:T(8,128)S(1)} %get-tuple-element.12.base, bf16[1024,256]{1,0:T(8,128)(2,1)S(1)} %get-tuple-element.13.fh, bf16[1024,256]{1,0:T(8,128)(2,1)S(1)} %get-tuple-element.14.fl, f32[2,128,128]{2,1,0:T(8,128)S(1)} %get-tuple-element.15.inv, ...), custom_call_target="tpu_custom_call" | custom-call | tf_op jit(solution)/shard_map/apply_panels/pallas_call | solution.py:535

commit v6 on v5

--- a/solution.py
+++ b/solution.py
@@ -25,21 +25,19 @@
 
 
 def send_all(count, me, source, slot, target, send_sem, recv_sem):
-    def step(q, carry):
-        @pl.when(q != me)
-        def _():
-            pltpu.make_async_remote_copy(
-                src_ref=source(q),
-                dst_ref=slot(me),
-                send_sem=send_sem.at[q],
-                recv_sem=recv_sem.at[me],
-                device_id=target(q),
-                device_id_type=MESH,
-            ).start()
-
+    def step(i, carry):
+        q = (me + i) % count
+        pltpu.make_async_remote_copy(
+            src_ref=source(q),
+            dst_ref=slot(me),
+            send_sem=send_sem.at[q],
+            recv_sem=recv_sem.at[me],
+            device_id=target(q),
+            device_id_type=MESH,
+        ).start()
         return carry
 
-    lax.fori_loop(0, count, step, 0)
+    lax.fori_loop(1, count, step, 0)
 
 
 def wait_all(count, me, source, slot, target, send_sem, recv_sem, sent=False):
@@ -214,7 +212,7 @@
     row_node = [n % NODES for n in found[4:]]
     keep_row = [[pat[p, n] == 1 for n in row_node] for p in range(2)]
 
-    for d in FAR_FIRST + (0,):
+    for d in FAR_FIRST[:4]:
         scatter(d, 0)
     recv_all(*d1_args)
     for t, (p, n) in enumerate(lead):
@@ -223,6 +221,8 @@
     rd2[z] = pd1[...]
     d2_args = (8, z, lambda q: pd1, lambda q: rd2.at[q], along, d2, e2)
     send_all(*d2_args)
+    for d in FAR_FIRST[4:] + (0,):
+        scatter(d, 0)
     for d in FAR_FIRST + (0,):
         scatter(d, 1)
 

time: 50.3 us -> 49.8 us (0.990)
    pallas_call x1, Pallas kernels: 48.2 us -> 47.6 us  [gather_tiles(): pl.pallas_call(comm_kernel, out_shape=(out(2, 8, W, W), out(8 * W, 2 * W,...]
where the time goes in v6:
time: 49.8 us; the launch traced here: 49.7 us
  Pallas kernels  49.7 us (100%)
    pallas_call x1, Pallas kernels, gather_tiles(): pl.pallas_call(comm_kernel, out_shape=(out(2, 8, W, W), out(8 * W, 2 * W,...  47.6 us
    pallas_call x1, Pallas kernels, apply_panels(): pl.pallas_call(apply_kernel, out_shape=jax.ShapeDtypeStruct((2, 8, W, W),...  2.03 us

profile of v6, /device:TPU:1, one launch (start us, length us, event | category | flops | bytes accessed | tf_op | source)
XLA Modules:
  0.0 49.7 jit_solution(6536286649728034877)
XLA Ops:
  0.0 47.6 %gather_tiles.1 = (f32[2,8,128,128]{3,2,1,0:T(8,128)S(1)}, bf16[1024,256]{1,0:T(8,128)(2,1)S(1)}, bf16[1024,256]{1,0:T(8,128)(2,1)S(1)}, f32[2,128,128]{2,1,0:T(...) custom-call(f32[2,8,128,128]{3,2,1,0:T(8,128)} %mat_hbm.1, s32[64]{0:T(128)} %co_hbm.1, ...), custom_call_target="tpu_custom_call" | custom-call | tf_op jit(solution)/shard_map/gather_tiles/pallas_call | solution.py:394
  47.7 2.0 %apply_panels.1 = f32[2,8,128,128]{3,2,1,0:T(8,128)} custom-call(f32[2,8,128,128]{3,2,1,0:T(8,128)S(1)} %get-tuple-element.12.base, bf16[1024,256]{1,0:T(8,128)(2,1)S(1)} %get-tuple-element.13.fh, bf16[1024,256]{1,0:T(8,128)(2,1)S(1)} %get-tuple-element.14.fl, f32[2,128,128]{2,1,0:T(8,128)S(1)} %get-tuple-element.15.inv, ...), custom_call_target="tpu_custom_call" | custom-call | tf_op jit(solution)/shard_map/apply_panels/pallas_call | solution.py:535

commit v7 on v6

--- a/solution.py
+++ b/solution.py
@@ -515,15 +515,15 @@
     gh = jnp.concatenate([g0h, g1h], axis=1)
     gl = jnp.concatenate([g0l, g1l], axis=1)
     copies = []
-    for s in range(0, 8, 2):
-        both = slice(W * s, W * s + 2 * W)
+    for s in range(0, 8, 4):
+        both = slice(W * s, W * s + 4 * W)
         step = nt16(fh[both], gh) + nt16(fl[both], gh) + nt16(fh[both], gl)
         for l in range(2):
-            for i in range(2):
+            for i in range(4):
                 old = base[l, s + i]
                 new = old - step[W * i : W * i + W, W * l : W * l + W]
                 buf[l, s + i] = jnp.where(flag(8 * l + s + i), new, old)
-            copy = pltpu.make_async_copy(buf.at[l, pl.ds(s, 2)], out.at[l, pl.ds(s, 2)], sem.at[l + s])
+            copy = pltpu.make_async_copy(buf.at[l, pl.ds(s, 4)], out.at[l, pl.ds(s, 4)], sem.at[l + s])
             copy.start()
             copies.append(copy)
     for copy in copies:

time: 49.8 us -> 49.9 us (level)
  no operation moved by 1% of the time
where the time goes in v7:
time: 49.9 us; the launch traced here: 49.8 us
  Pallas kernels  49.8 us (100%)
    pallas_call x1, Pallas kernels, gather_tiles(): pl.pallas_call(comm_kernel, out_shape=(out(2, 8, W, W), out(8 * W, 2 * W,...  47.6 us
    pallas_call x1, Pallas kernels, apply_panels(): pl.pallas_call(apply_kernel, out_shape=jax.ShapeDtypeStruct((2, 8, W, W),...  2.19 us

profile of v7, /device:TPU:1, one launch (start us, length us, event | category | flops | bytes accessed | tf_op | source)
XLA Modules:
  0.0 49.8 jit_solution(12620533815305940413)
XLA Ops:
  0.0 47.6 %gather_tiles.1 = (f32[2,8,128,128]{3,2,1,0:T(8,128)S(1)}, bf16[1024,256]{1,0:T(8,128)(2,1)S(1)}, bf16[1024,256]{1,0:T(8,128)(2,1)S(1)}, f32[2,128,128]{2,1,0:T(...) custom-call(f32[2,8,128,128]{3,2,1,0:T(8,128)} %mat_hbm.1, s32[64]{0:T(128)} %co_hbm.1, ...), custom_call_target="tpu_custom_call" | custom-call | tf_op jit(solution)/shard_map/gather_tiles/pallas_call | solution.py:394
  47.7 2.2 %apply_panels.1 = f32[2,8,128,128]{3,2,1,0:T(8,128)} custom-call(f32[2,8,128,128]{3,2,1,0:T(8,128)S(1)} %get-tuple-element.12.base, bf16[1024,256]{1,0:T(8,128)(2,1)S(1)} %get-tuple-element.13.fh, bf16[1024,256]{1,0:T(8,128)(2,1)S(1)} %get-tuple-element.14.fl, f32[2,128,128]{2,1,0:T(8,128)S(1)} %get-tuple-element.15.inv, ...), custom_call_target="tpu_custom_call" | custom-call | tf_op jit(solution)/shard_map/apply_panels/pallas_call | solution.py:535
